TPU v7x, 32 devices: a whole 2x2x4 slice. The times are simulated.
32 devices in a mesh: pipe: 2 (over core), dp: 16 (over z, y, x).
Axes of the slice: x: 2, y: 2, z: 4, core: 2. Of those that a mesh axis runs over, the one named last changes fastest.
Arguments:
- layer_input: bfloat16 [2, 16, 512, 768], P('pipe', 'dp'), may hold values from -100 to 100
- saved_qkv: bfloat16 [2, 16, 512, 2304], P('pipe', 'dp'), may hold values from -27 to 27
- ln_gain: float32 [2, 768], P('pipe'), may hold values from 0.1 to 1.9
- layer_weights: bfloat16 [2, 768, 3072], P('pipe', 'dp'), may hold values from -0.21875 to 0.21875
- rand_blocks: int32 [2, 12, 6, 3], P('pipe'), may hold values from 1 to 6, as said below
- out_grad: bfloat16 [16, 512, 768], P('dp'), may hold values from -6 to 6
Outputs:
- grad_inputs: bfloat16 [2, 16, 512, 768], P('pipe', 'dp')
- grad_weights: float32 [2, 768, 3072], P('pipe', 'dp')
Inputs may be any that keep to these rules, and one draw needn't show every extreme that they name: `rand_blocks`: for each layer, head and middle block i (entry i - 1), 3 different blocks other than i - 1, i and i + 1.
All inputs are finite; a program needn't handle non-finite values.
Results may differ from a plain program's by a relative error of at most 0.0072.
Values may be sent and summed in bfloat16 or wider, within the bound.
No kernel may reach another device: no remote copies, remote signals or barrier semaphores. Data moves between devices by JAX's collectives and lax.ppermute only.
A program may use at most 192 MiB of HBM per device.

v0:
```python
import math

import jax
import jax.numpy as jnp
from jax import lax
from jax.experimental import pallas as pl
from jax.experimental.pallas import tpu as pltpu
from jax.sharding import PartitionSpec as P

HEADS = 12
HEAD_DIM = 64
BLOCK = 64
INNER = HEADS * HEAD_DIM
PAIR = 2 * HEAD_DIM
PAIRS = HEADS // 2
EPSILON = 1e-05
NEGATIVE = -1e30
SCALE = HEAD_DIM ** (-0.5)
QKV_COLUMNS = (0, 3 * INNER)
OUT_COLUMNS = (3 * INNER, 4 * INNER)
MEGABYTE = 1024 * 1024
F32 = jnp.float32
BF16 = jnp.bfloat16
ANY = pl.BlockSpec(memory_space=pl.ANY)
SMEM = pl.BlockSpec(memory_space=pltpu.SMEM)
HBM = pl.BlockSpec(memory_space=pltpu.HBM)
VMEM = pl.BlockSpec(memory_space=pltpu.VMEM)


def dot_nn(left, right):
    return lax.dot_general(left, right, (((1,), (0,)), ((), ())), preferred_element_type=F32)


def dot_nt(left, right):
    return lax.dot_general(left, right, (((1,), (1,)), ((), ())), preferred_element_type=F32)


def dot_tn(left, right):
    return lax.dot_general(left, right, (((0,), (0,)), ((), ())), preferred_element_type=F32)


def call(body, out_shape, in_specs, out_specs, scratch, megabytes, aliases=None):
    return pl.pallas_call(
        body,
        out_shape=out_shape,
        in_specs=in_specs,
        out_specs=out_specs,
        scratch_shapes=scratch,
        input_output_aliases=aliases or {},
        compiler_params=pltpu.CompilerParams(vmem_limit_bytes=megabytes * MEGABYTE),
    )


def shape(dims, dtype=BF16):
    return jax.ShapeDtypeStruct(dims, dtype)


def start_all(copies):
    for copy in copies:
        copy.start()
    return copies


def wait_all(copies):
    for copy in copies:
        copy.wait()


def scaled(value):
    return (value.astype(F32) * SCALE).astype(BF16)


def half_lanes(like, half):
    lane = lax.broadcasted_iota(jnp.int32, like.shape, 1)
    return (lane >= half * HEAD_DIM) & (lane < (half + 1) * HEAD_DIM)


def columns_of(pair, group, width):
    return pl.ds(pl.multiple_of(group * width + pair * PAIR, PAIR), PAIR)


def skipped_block(draws, middle, blocks):
    near = range(3, blocks - 1) if middle == 0 else range(1, blocks - 3)
    return sum(near) - jnp.sum(draws[middle : middle + 1], axis=1, keepdims=True)


def forward_pair(pair, index, width, rand_ref, qkv_v):
    queries = scaled(qkv_v[:, columns_of(index, 0, width)])
    keys = qkv_v[:, columns_of(index, 1, width)]
    values_t = qkv_v[:, columns_of(index, 2, width)].T
    blocks = queries.shape[0] // BLOCK
    row_block = lax.broadcasted_iota(jnp.int32, queries.shape, 0) // BLOCK
    lane = lax.broadcasted_iota(jnp.int32, queries.shape, 1)
    probs, parts = [], []
    for half in range(2):
        own = half_lanes(keys, half)
        low = skipped_block(rand_ref[2 * pair + half], 0, blocks)
        high = skipped_block(rand_ref[2 * pair + half], blocks - 3, blocks)
        first = (1 - half) * HEAD_DIM
        marks = ((lane == first) & (row_block == low)) | (
            (lane == first + 1) & (row_block == high)
        )
        bars = ((lane == first) & (row_block == 1)) | (
            (lane == first + 1) & (row_block == blocks - 2)
        )
        key_side = jnp.where(own, keys, jnp.where(marks, 1.0, 0.0).astype(BF16))
        query_side = jnp.where(own, queries, jnp.where(bars, NEGATIVE, 0.0).astype(BF16))
        scores = dot_nt(key_side, query_side)
        powers = jnp.exp(scores - jnp.max(scores, axis=0, keepdims=True))
        inverse = 1.0 / jnp.sum(powers, axis=0, keepdims=True)
        weights = (powers * inverse).astype(BF16)
        probs.append(weights)
        parts.append(dot_nn(values_t[half * HEAD_DIM : (half + 1) * HEAD_DIM], weights))
    return probs, jnp.concatenate(parts, axis=0).T.astype(BF16)


def is_top():
    return lax.axis_index("pipe") == lax.axis_size("pipe") - 1


def forward_body(pairs, aliased, rand_ref, qkv, *refs):
    @pl.when(is_top() if aliased else jnp.logical_not(is_top()))
    def _():
        forward_part(pairs, rand_ref, qkv, *refs[aliased:])


def forward_part(pairs, rand_ref, qkv, weights, context, kept, qkv_v, p_v, context_v, sems):
    first, count = pairs
    width = count * PAIR
    loads, stores = [], []
    for group in range(3):
        at = pl.ds(group * INNER + first * PAIR, width)
        held = qkv_v.at[:, pl.ds(group * width, width)]
        loads.append(pltpu.make_async_copy(qkv.at[:, at], held, sems.at[group]))
        stores.append(pltpu.make_async_copy(held, kept.at[:, at], sems.at[3 + group]))
    wait_all(start_all(loads))
    start_all(stores)

    def p_copy(index):
        held, at = pl.ds(2 * index, 2), pl.ds(2 * (first + index), 2)
        return pltpu.make_async_copy(p_v.at[held], weights.at[at], sems.at[7 + index])

    def one_pair(index, unused):
        probs, context_part = forward_pair(first + index, index, width, rand_ref, qkv_v)
        for half in range(2):
            p_v[2 * index + half] = probs[half]
        context_v[:, columns_of(index, 0, width)] = context_part
        p_copy(index).start()
        return unused

    lax.fori_loop(0, count, one_pair, 0)
    target = context.at[:, pl.ds(first * PAIR, width)]
    stores += start_all([pltpu.make_async_copy(context_v, target, sems.at[6])])
    stores += [p_copy(index) for index in range(count)]
    wait_all(stores)


def forward(pairs, rand, qkv, carry):
    first, count = pairs
    length = qkv.shape[0]
    carry = list(carry or ())
    aliases = {2 + index: index for index in range(len(carry))}

    def body(*refs):
        forward_body(pairs, len(carry), *refs)

    return call(
        body,
        (shape((HEADS, length, length)), shape((length, INNER)), shape((length, 3 * INNER))),
        [VMEM, HBM] + [ANY] * len(carry),
        (ANY,) * 3,
        [
            pltpu.VMEM((length, 3 * PAIR * count), BF16),
            pltpu.VMEM((2 * count, length, length), BF16),
            pltpu.VMEM((length, PAIR * count), BF16),
            pltpu.SemaphoreType.DMA((7 + count,)),
        ],
        22 if count > 2 else 14,
        aliases,
    )(rand, qkv, *carry)


def statistics(x):
    values = x.astype(F32)
    centred = values - jnp.mean(values, axis=-1, keepdims=True)
    inverse = lax.rsqrt(jnp.mean(centred * centred, axis=-1, keepdims=True) + EPSILON)
    return centred * inverse, inverse


def norm_body(x_ref, gain_ref, out_ref):
    standard, _ = statistics(x_ref[...])
    out_ref[...] = (standard * gain_ref[...]).astype(BF16).T


def normed_transposed(x, gain):
    length, width = x.shape
    return call(norm_body, shape((width, length)), [VMEM, VMEM], VMEM, [], 10)(x, gain)


def weight_copies(pieces, layout, target, sems, wanted):
    low, high = wanted
    position = lax.axis_index("dp")
    copies = []
    for (first, second), order, (start, stop) in zip(pieces, *layout):
        left, right = max(start, low), min(stop, high)
        if left >= right:
            continue
        half = first.shape[0]
        rows = first.shape[1]
        for slot, offset in enumerate(order):
            source = first if slot < half else second
            row = pl.multiple_of((position ^ offset) * rows, math.gcd(rows, 16))
            copies.append(
                pltpu.make_async_copy(
                    source.at[slot % half, :, pl.ds(left - start, right - left)],
                    target.at[pl.ds(row, rows), pl.ds(left - low, right - left)],
                    sems.at[len(copies)],
                )
            )
    return copies


def copy_count(layout, wanted):
    return sum(
        len(order)
        for order, (start, stop) in zip(*layout)
        if max(start, wanted[0]) < min(stop, wanted[1])
    )


def is_turn(turn):
    return lax.axis_index("pipe") == lax.axis_size("pipe") - 1 - turn


def zip_pieces(refs, layout):
    count = 2 * len(layout[1])
    return list(zip(refs[:count:2], refs[1:count:2])), refs[count:]


def flat_pieces(gathered):
    return [piece for pair in gathered for piece in pair]


def backward_pair(pair, qkv_v, p_v, context_v, gc_v, grad_v):
    queries = scaled(qkv_v[:, columns_of(pair, 0, INNER)])
    keys_t = scaled(qkv_v[:, columns_of(pair, 1, INNER)]).T
    values = qkv_v[:, columns_of(pair, 2, INNER)]
    grads = gc_v[:, columns_of(pair, 0, INNER)]
    zero = jnp.zeros_like(grads)
    product_t = (grads.astype(F32) * context_v[:, columns_of(pair, 0, INNER)].astype(F32)).T
    key_grad = value_grad = None
    query_parts = []
    for half in range(2):
        rows = slice(half * HEAD_DIM, (half + 1) * HEAD_DIM)
        own = half_lanes(grads, half)
        probs = p_v[2 * pair + half]
        delta = jnp.sum(product_t[rows], axis=0, keepdims=True)
        weight_grad = dot_nt(jnp.where(own, values, zero), grads)
        score_grad = (probs.astype(F32) * (weight_grad - delta)).astype(BF16)
        key_part = dot_nn(score_grad, jnp.where(own, queries, zero))
        value_part = dot_nn(probs, jnp.where(own, grads, zero))
        key_grad = key_part if half == 0 else key_grad + key_part
        value_grad = value_part if half == 0 else value_grad + value_part
        query_parts.append(dot_nn(keys_t[rows], score_grad))
    grad_v[:, columns_of(pair, 0, INNER)] = jnp.concatenate(query_parts, axis=0).T.astype(BF16)
    grad_v[:, columns_of(pair, 1, INNER)] = key_grad.astype(BF16)
    grad_v[:, columns_of(pair, 2, INNER)] = value_grad.astype(BF16)


def input_gradient(upper_v, grad_v, x_v, w_v, gain_ref):
    grad_standard = dot_nt(grad_v[...], w_v[...]) * gain_ref[...]
    standard, inverse = statistics(x_v[...])
    correction = jnp.mean(grad_standard, axis=-1, keepdims=True) + standard * jnp.mean(
        grad_standard * standard, axis=-1, keepdims=True
    )
    return (upper_v[...].astype(F32) + inverse * (grad_standard - correction)).astype(BF16)


def section_body(layout, turn, aliased, with_input, *refs):
    gain_ref, received, top, x, qkv, weights, context = refs[:7]
    pieces, refs = zip_pieces(refs[7:], layout)
    refs = refs[aliased:]
    upper_out, grad_out, input_out = refs[:3] if with_input else (*refs[:2], None)
    refs = refs[3 if with_input else 2 :]
    upper_v, out_w, gc_v, grad_v, sems, w_sems = refs[:6]

    @pl.when(is_turn(turn))
    def _():
        w_copies = start_all(weight_copies(pieces, layout, out_w, w_sems, OUT_COLUMNS))
        top_copy = pltpu.make_async_copy(top, upper_v, sems.at[2])
        pl.when(is_top())(top_copy.start)

        @pl.when(jnp.logical_not(is_top()))
        def _():
            upper_v[...] = received[...]

        late = []
        if with_input:
            x_v, qkv_w, out_v, qkv_sems = refs[6:]
            late = weight_copies(pieces, layout, qkv_w, qkv_sems, QKV_COLUMNS)
            late.append(pltpu.make_async_copy(x, x_v, sems.at[3]))
        pl.when(is_top())(top_copy.wait)
        stores = start_all([pltpu.make_async_copy(upper_v, upper_out, sems.at[0])])
        wait_all(w_copies)
        start_all(late)
        gc_v[...] = dot_nn(upper_v[...], out_w[...]).astype(BF16)

        def one_pair(pair, unused):
            backward_pair(pair, qkv, weights, context, gc_v, grad_v)
            return unused

        lax.fori_loop(0, PAIRS, one_pair, 0, unroll=2)
        stores += start_all([pltpu.make_async_copy(grad_v, grad_out, sems.at[1])])
        if with_input:
            wait_all(late)
            out_v[...] = input_gradient(upper_v, grad_v, x_v, qkv_w, gain_ref)
            stores += start_all([pltpu.make_async_copy(out_v, input_out, sems.at[4])])
        wait_all(stores)


def section_backward(turn, with_input, gain, received, top, x, saved, gathered, layout, carry):
    length, width = x.shape
    weights, context, qkv = saved
    inputs = [gain, received, top, x, qkv, weights, context]
    specs = [VMEM, VMEM, ANY, ANY, VMEM, VMEM, VMEM]
    inputs = inputs + flat_pieces(gathered)
    outs = [shape((length, width)), shape((length, 3 * INNER))]
    outs = outs + [shape((length, width))] * with_input
    aliases = {}
    if carry is not None:
        aliases = {len(inputs) + index: index for index in range(len(outs))}
        inputs = inputs + list(carry[: len(outs)])

    def body(*refs):
        section_body(layout, turn, len(aliases), with_input, *refs)

    scratch = [
        pltpu.VMEM((length, width), BF16),
        pltpu.VMEM((width, INNER), BF16),
        pltpu.VMEM((length, INNER), BF16),
        pltpu.VMEM((length, 3 * INNER), BF16),
        pltpu.SemaphoreType.DMA((5,)),
        pltpu.SemaphoreType.DMA((copy_count(layout, OUT_COLUMNS),)),
    ]
    if with_input:
        scratch += [
            pltpu.VMEM((length, width), BF16),
            pltpu.VMEM((width, 3 * INNER), BF16),
            pltpu.VMEM((length, width), BF16),
            pltpu.SemaphoreType.DMA((copy_count(layout, QKV_COLUMNS),)),
        ]
    return call(
        body,
        tuple(outs),
        specs + [ANY] * (len(inputs) - len(specs)),
        (ANY,) * len(outs),
        scratch,
        24 if with_input else 16,
        aliases,
    )(*inputs)


def project_body(layout, turn, gain_ref, upper, grad, x, *refs):
    pieces, refs = zip_pieces(refs, layout)
    out, x_v, w_v, out_v, sems, w_sems = refs[1:]

    @pl.when(is_turn(turn))
    def _():
        copies = weight_copies(pieces, layout, w_v, w_sems, QKV_COLUMNS)
        copies.append(pltpu.make_async_copy(x, x_v, sems.at[0]))
        wait_all(start_all(copies))
        out_v[...] = input_gradient(upper, grad, x_v, w_v, gain_ref)
        wait_all(start_all([pltpu.make_async_copy(out_v, out, sems.at[1])]))


def project(turn, gain, upper, x, grad, gathered, layout, carry):
    length, width = x.shape
    inputs = [gain, upper, grad, x] + flat_pieces(gathered) + [carry]

    def body(*refs):
        project_body(layout, turn, *refs)

    return call(
        body,
        shape((length, width)),
        [VMEM] * 3 + [ANY] * (len(inputs) - 3),
        ANY,
        [
            pltpu.VMEM((length, width), BF16),
            pltpu.VMEM((width, 3 * INNER), BF16),
            pltpu.VMEM((length, width), BF16),
            pltpu.SemaphoreType.DMA((2,)),
            pltpu.SemaphoreType.DMA((copy_count(layout, QKV_COLUMNS),)),
        ],
        16,
        {len(inputs) - 1: 0},
    )(*inputs)


def term_body(layout, rows, normed, upper, grad, context, *refs):
    position = lax.axis_index("dp")
    count = 2 * len(layout[1])
    outs, (upper_t, normed_v, upper_v) = refs[:count], refs[count:]
    upper_t[...] = upper[...].T
    for chunk, (order, (start, stop)) in enumerate(zip(*layout)):
        half = len(order) // 2
        for slot, offset in enumerate(order):
            row = pl.multiple_of((position ^ offset) * rows, math.gcd(rows, 16))
            own, source = pl.ds(slot * rows, rows), pl.ds(row, rows)
            if start < 3 * INNER:
                normed_v[own] = normed[source]
            if stop > 3 * INNER:
                upper_v[own] = upper_t[source]
        for out, side in ((outs[2 * chunk + 1], 1), (outs[2 * chunk], 0)):
            at = slice(side * half * rows, (side + 1) * half * rows)

            def store(value, low, high, out=out):
                out[:, :, low - start : high - start] = value.astype(BF16).reshape(
                    half, rows, high - low
                )

            if start < 3 * INNER:
                high = min(stop, 3 * INNER)
                store(dot_nn(normed_v[at], grad[:, start:high]), start, high)
            if stop > 3 * INNER:
                low = max(start, 3 * INNER)
                part = context[:, low - 3 * INNER : stop - 3 * INNER]
                store(dot_nn(upper_v[at], part), low, stop)


def weight_terms(normed, upper, grad, context, rows, layout):
    width, length = normed.shape
    inputs = [normed, upper, grad, context]
    orders, columns = layout
    count = len(orders[0])
    outs = tuple(
        shape((count // 2, rows, stop - start)) for start, stop in columns for _ in range(2)
    )

    def body(*refs):
        term_body(layout, rows, *refs)

    return call(
        body,
        outs,
        [VMEM] * len(inputs),
        (VMEM,) * len(outs),
        [
            pltpu.VMEM((width, length), BF16),
            pltpu.VMEM((width, length), BF16),
            pltpu.VMEM((width, length), BF16),
        ],
        24,
    )(*inputs)


def bit_orders(count, free):
    bits = [1 << b for b in range(count.bit_length() - 1)]
    near, far = bits[:free], bits[free:][::-1]
    return [far + near[c:] + near[:c] for c in range(free)]


def slot_offsets(order):
    offsets = [0]
    for bit in order:
        offsets = offsets + [offset ^ bit for offset in offsets]
    return offsets


def exchange_layout(total, orders):
    wide = total // len(orders)
    columns = [(c * wide, (c + 1) * wide) for c in range(len(orders))]
    return [slot_offsets(order) for order in orders], columns


def across(value, bit):
    count = lax.axis_size("dp")
    return lax.ppermute(value, "dp", [(source, source ^ bit) for source in range(count)])


class Gather:
    def __init__(self, shard, orders):
        self.orders = orders
        self.steps = len(orders[0])
        self.layout = exchange_layout(shard.shape[1], orders)
        self.held = [shard[None]]
        self.step = 0
        self.final = None

    def advance(self):
        step, chunks = self.step, len(self.orders)
        if len(self.held) == 1 and len({order[step] for order in self.orders}) > 1:
            self.held = [self.held[0][:, :, start:stop] for start, stop in self.layout[1]]
        got = [across(held, order[step]) for held, order in zip(self.held, self.orders)]
        self.step = step + 1
        if self.step < self.steps:
            self.held = [jnp.concatenate(pair, axis=0) for pair in zip(self.held, got)]
        else:
            if len(got) < chunks:
                self.held = [self.held[0][:, :, start:stop] for start, stop in self.layout[1]]
                got = [got[0][:, :, start:stop] for start, stop in self.layout[1]]
            self.final = list(zip(self.held, got))

    def after(self, *values):
        self.held, values = lax.optimization_barrier((self.held, values))
        return values


def scatter_rows(terms, orders, scale):
    chunk_count = len(orders)
    steps = len(orders[0])
    kept = [[terms[2 * c]] for c in range(chunk_count)]
    outgoing = [terms[2 * c + 1] for c in range(chunk_count)]
    for step in reversed(range(steps)):
        if step == 0 and all(order[0] == orders[0][0] for order in orders):
            break
        got = [across(outgoing[c], orders[c][step]) for c in range(chunk_count)]
        for c in range(chunk_count):
            kept[c].append(got[c])
        if step:
            half = 1 << (step - 1)
            for c in range(chunk_count):
                total = sum(part[half : 2 * half].astype(F32) for part in kept[c])
                outgoing[c] = total.astype(BF16)
    total = jnp.concatenate(
        [sum(part[0].astype(F32) for part in kept[c]) for c in range(chunk_count)], axis=-1
    )
    if len(kept[0]) <= steps:
        last = across(jnp.concatenate([out[0] for out in outgoing], axis=-1), orders[0][0])
        total = total + last.astype(F32)
    return total * scale


def on_device(layer_input, saved_qkv, ln_gain, layer_weights, rand_blocks, out_grad):
    sections = lax.axis_size("pipe")
    replicas = lax.axis_size("dp")
    x, qkv, top, shard = layer_input[0, 0], saved_qkv[0, 0], out_grad[0], layer_weights[0]
    rand = rand_blocks[0]
    rows, total = shard.shape

    orders = bit_orders(replicas, 3)
    gather = Gather(shard, orders)
    saved = forward((0, PAIRS), rand, qkv, None)
    saved = gather.after(*saved)
    gather.advance()
    share = PAIRS // 3
    for part in range(3):
        saved = forward((part * share, share), rand, qkv, saved)
        if part == 0:
            normed = normed_transposed(x, ln_gain)
            *saved, normed = gather.after(*saved, normed)
            gather.advance()
        elif part == 1:
            gather.advance()
            saved = gather.after(*saved)
            gather.advance()
    while gather.final is None:
        gather.advance()
    pieces = (gather.final, gather.layout)

    received = top
    carry = None
    for turn in range(sections):
        below = turn + 1 < sections
        kept = section_backward(turn, below, ln_gain, received, top, x, saved, *pieces, carry)
        carry = [*kept, *(carry or kept)[len(kept) :]]
        if below:
            received = lax.ppermute(
                carry[2], "pipe", [(source, source - 1) for source in range(1, sections)]
            )
    upper, grad, grad_input = carry
    terms = weight_terms(
        normed, upper, grad, saved[1], rows, exchange_layout(total, orders)
    )
    summed = scatter_rows(terms, orders, 1.0 / replicas)
    grad_input = project(sections - 1, ln_gain, upper, x, grad, *pieces, grad_input)
    return (grad_input[None, None], summed[None])


def solution(mesh):
    placed = (
        P("pipe", "dp", None, None),
        P("pipe", "dp", None, None),
        P("pipe", None),
        P("pipe", "dp", None),
        P("pipe", None, None, None),
        P("dp", None, None),
    )
    return jax.shard_map(
        on_device,
        mesh=mesh,
        in_specs=placed,
        out_specs=(P("pipe", "dp", None, None), P("pipe", "dp", None)),
        check_vma=False,
    )
```

profile of v0, /device:TPU:0, one launch (start us, length us, event | category | flops | bytes accessed | tf_op | source)
XLA Modules:
  0.0 126.3 jit_solution(15285346360067779159)
XLA Ops:
  0.6 0.8 copy.20
  1.5 1.7 %copy-done = bf16[1,1,512,2304]{3,2,1,0:T(8,128)(2,1)S(1)} copy-done((bf16[1,1,512,2304]{3,2,1,0:T(8,128)(2,1)S(1)}, bf16[1,1,512,2304]{3,2,1,0:T(8,128)(2,1)}, u32[]{:S(2)}) %copy-start) | copy-done | bytes 2359320
  3.1 9.9 %shard_map.77 = (bf16[12,512,512]{2,1,0:T(8,128)(2,1)S(1)}, bf16[512,768]{1,0:T(8,128)(2,1)S(1)}, bf16[512,2304]{1,0:T(8,128)(2,1)S(1)}) custom-call(s32[12,6,3]{2,1,0:T(8,128)S(1)} %bitcast.30, bf16[512,2304]{1,0:T(8,128)(2,1)S(1)} %bitcast.19), custom_call_target="tpu_custom_call" | custom-call | tf_op jit(solution)/shard_map/pallas_call | solution.py:167
  13.0 4.1 %collective-permute-start = (bf16[1,48,3072]{2,1,0:T(8,128)(2,1)}, bf16[1,48,3072]{2,1,0:T(8,128)(2,1)S(1)}, u32[]{:S(2)}, u32[]{:S(2)}) collective-permute-start(bf16[1,48,3072]{2,1,0:T(8,128)(2,1)} %param.9), channel_id=1, source_target_pairs={{0,8},{1,9},{2,10},{3,11},{4,12},{5,13},{6,14},{7,15},{8,0},{9,1},... | collective-permute-start | bytes 884744 | tf_op jit(solution)/shard_map/ppermute | solution.py:478
  17.1 1.1 copy-done.2
  18.2 0.7 shard_map.79.refs_0_
  19.0 6.3 %collective-permute-done = bf16[1,48,3072]{2,1,0:T(8,128)(2,1)S(1)} collective-permute-done((bf16[1,48,3072]{2,1,0:T(8,128)(2,1)}, bf16[1,48,3072]{2,1,0:T(8,128)(2,1)S(1)}, u32[]{:S(2)}, u32[]{:S(2)}) %collective-permute-start) | collective-permute-done | bytes 294944 | tf_op jit(solution)/shard_map/ppermute | solution.py:478
  25.4 1.1 collective-permute-start.5
  26.5 1.5 %collective-permute-start.3 = (bf16[2,48,1024]{2,1,0:T(8,128)(2,1)S(1)}, bf16[2,48,1024]{2,1,0:T(8,128)(2,1)S(1)}, u32[]{:S(2)}, u32[]{:S(2)}) collective-permute-start(bf16[2,48,1024]{2,1,0:T(8,128)(2,1)S(1)} %get-tuple-element.85), channel_id=1, source_target_pairs={{0,2},{1,3},{2,0},{3,1},{4,6},{5,7},{6,4},{7,5},{8,10},{9,11},{10,... | collective-permute-start | bytes 589832 | tf_op jit(solution)/shard_map/ppermute | solution.py:478
  28.0 1.5 %collective-permute-start.1 = (bf16[2,48,1024]{2,1,0:T(8,128)(2,1)S(1)}, bf16[2,48,1024]{2,1,0:T(8,128)(2,1)S(1)}, u32[]{:S(2)}, u32[]{:S(2)}) collective-permute-start(bf16[2,48,1024]{2,1,0:T(8,128)(2,1)S(1)} %get-tuple-element.86), channel_id=1, source_target_pairs={{0,1},{1,0},{2,3},{3,2},{4,5},{5,4},{6,7},{7,6},{8,9},{9,8},{10,11... | collective-permute-start | bytes 589832 | tf_op jit(solution)/shard_map/ppermute | solution.py:478
  29.5 2.0 %collective-permute-done.5 = bf16[2,48,1024]{2,1,0:T(8,128)(2,1)S(1)} collective-permute-done((bf16[2,48,1024]{2,1,0:T(8,128)(2,1)S(1)}, bf16[2,48,1024]{2,1,0:T(8,128)(2,1)S(1)}, u32[]{:S(2)}, u32[]{:S(2)}) %collective-permute-start.5) | collective-permute-done | bytes 196640 | tf_op jit(solution)/shard_map/ppermute | solution.py:478
  31.6 1.7 %collective-permute-start.6 = (bf16[4,48,1024]{2,1,0:T(8,128)(2,1)S(1)}, bf16[4,48,1024]{2,1,0:T(8,128)(2,1)S(1)}, u32[]{:S(2)}, u32[]{:S(2)}) collective-permute-start(bf16[4,48,1024]{2,1,0:T(8,128)(2,1)S(1)} %pad_maximum_fusion.6), channel_id=1, source_target_pairs={{0,1},{1,0},{2,3},{3,2},{4,5},{5,4},{6,7},{7,6},{8,9},{9,8},{10,11... | collective-permute-start | bytes 1179656 | tf_op jit(solution)/shard_map/ppermute | solution.py:478
  33.4 0.5 collective-permute-start.4
  33.9 0.3 collective-permute-done.1
  34.2 1.3 %collective-permute-start.2 = (bf16[4,48,1024]{2,1,0:T(8,128)(2,1)S(1)}, bf16[4,48,1024]{2,1,0:T(8,128)(2,1)S(1)}, u32[]{:S(2)}, u32[]{:S(2)}) collective-permute-start(bf16[4,48,1024]{2,1,0:T(8,128)(2,1)S(1)} %pad_maximum_fusion.4), channel_id=1, source_target_pairs={{0,2},{1,3},{2,0},{3,1},{4,6},{5,7},{6,4},{7,5},{8,10},{9,11},{10,... | collective-permute-start | bytes 1179656 | tf_op jit(solution)/shard_map/ppermute | solution.py:478
  35.6 8.1 %collective-permute-done.6 = bf16[4,48,1024]{2,1,0:T(8,128)(2,1)S(1)} collective-permute-done((bf16[4,48,1024]{2,1,0:T(8,128)(2,1)S(1)}, bf16[4,48,1024]{2,1,0:T(8,128)(2,1)S(1)}, u32[]{:S(2)}, u32[]{:S(2)}) %collective-permute-start.6) | collective-permute-done | bytes 393248 | tf_op jit(solution)/shard_map/ppermute | solution.py:478
  43.8 1.6 %collective-permute-done.4 = bf16[4,48,1024]{2,1,0:T(8,128)(2,1)S(1)} collective-permute-done((bf16[4,48,1024]{2,1,0:T(8,128)(2,1)S(1)}, bf16[4,48,1024]{2,1,0:T(8,128)(2,1)S(1)}, u32[]{:S(2)}, u32[]{:S(2)}) %collective-permute-start.4) | collective-permute-done | bytes 393248 | tf_op jit(solution)/shard_map/ppermute | solution.py:478
  45.5 0.9 collective-permute-done.2
  46.4 1.5 %collective-permute-start.7 = (bf16[8,48,1024]{2,1,0:T(8,128)(2,1)S(1)}, bf16[8,48,1024]{2,1,0:T(8,128)(2,1)S(1)}, u32[]{:S(2)}, u32[]{:S(2)}) collective-permute-start(bf16[8,48,1024]{2,1,0:T(8,128)(2,1)S(1)} %pad_maximum_fusion.refs_7_.refs_4_), channel_id=1, source_target_pairs={{0,4},{1,5},{2,6},{3,7},{4,0},{5,1},{6,2},{7,3},{8,12},{9,13},{10,... | collective-permute-start | bytes 2359304 | tf_op jit(solution)/shard_map/ppermute | solution.py:478
  47.9 1.2 collective-permute-start.8
  49.2 0.9 collective-permute-start.9
  50.1 8.4 %collective-permute-done.7.refs_8_.refs_5_ = bf16[8,48,1024]{2,1,0:T(8,128)(2,1)S(1)} collective-permute-done((bf16[8,48,1024]{2,1,0:T(8,128)(2,1)S(1)}, bf16[8,48,1024]{2,1,0:T(8,128)(2,1)S(1)}, u32[]{:S(2)}, u32[]{:S(2)}) %collective-permute-start.7) | collective-permute-done | bytes 786464 | tf_op jit(solution)/shard_map/ppermute | solution.py:478
  58.5 1.4 %collective-permute-done.8.refs_10_.refs_7_ = bf16[8,48,1024]{2,1,0:T(8,128)(2,1)S(1)} collective-permute-done((bf16[8,48,1024]{2,1,0:T(8,128)(2,1)S(1)}, bf16[8,48,1024]{2,1,0:T(8,128)(2,1)S(1)}, u32[]{:S(2)}, u32[]{:S(2)}) %collective-permute-start.8) | collective-permute-done | bytes 786464 | tf_op jit(solution)/shard_map/ppermute | solution.py:478
  59.9 1.2 collective-permute-done.9.refs_12_.refs_9_
  61.1 0.6 shard_map.82
  61.8 1.3 %collective-permute-start.10 = (bf16[512,768]{1,0:T(8,128)(2,1)}, bf16[512,768]{1,0:T(8,128)(2,1)S(1)}, u32[]{:S(2)}, u32[]{:S(2)}) collective-permute-start(bf16[512,768]{1,0:T(8,128)(2,1)} %get-tuple-element.66.refs_10_), channel_id=1, source_target_pairs={{16,0},{17,1},{18,2},{19,3},{20,4},{21,5},{22,6},{23,7},{24,8},{25... | collective-permute-start | bytes 2359304 | tf_op jit(solution)/shard_map/ppermute | solution.py:568
  63.1 3.1 %collective-permute-done.10.refs_1_ = bf16[512,768]{1,0:T(8,128)(2,1)S(1)} collective-permute-done((bf16[512,768]{1,0:T(8,128)(2,1)}, bf16[512,768]{1,0:T(8,128)(2,1)S(1)}, u32[]{:S(2)}, u32[]{:S(2)}) %collective-permute-start.10) | collective-permute-done | bytes 786464 | tf_op jit(solution)/shard_map/ppermute | solution.py:568
  66.2 9.5 %shard_map.83 = (bf16[512,768]{1,0:T(8,128)(2,1)S(1)}, bf16[512,2304]{1,0:T(8,128)(2,1)S(1)}) custom-call(f32[1,768]{1,0:T(1,128)S(1)} %copy-done.5, bf16[512,768]{1,0:T(8,128)(2,1)S(1)} %collective-permute-done.10.refs_1_, bf16[512,768]{1,0:T(8,128)(2,1)S(1)} %bitcast.29, ...), custom_call_target="tpu_custom_call", output_to_operand_aliasing={{0}: (13, {}), {1}: (14, {})} | custom-call | tf_op jit(solution)/shard_map/pallas_call | solution.py:352
  75.6 2.6 %shard_map.85 = (bf16[8,48,1024]{2,1,0:T(8,128)(2,1)S(1)}, bf16[8,48,1024]{2,1,0:T(8,128)(2,1)S(1)}, bf16[8,48,1024]{2,1,0:T(8,128)(2,1)S(1)}, bf16[8,48,1024]{2...) custom-call(bf16[768,512]{1,0:T(8,128)(2,1)S(1)} %shard_map.79.refs_0_, ...), custom_call_target="tpu_custom_call" | custom-call | tf_op jit(solution)/shard_map/pallas_call | solution.py:443
  78.3 0.7 collective-permute-start.11
  79.0 0.7 collective-permute-start.14
  79.7 1.0 collective-permute-start.17
  80.7 13.8 %collective-permute-done.11 = bf16[8,48,1024]{2,1,0:T(8,128)(2,1)S(1)} collective-permute-done((bf16[8,48,1024]{2,1,0:T(8,128)(2,1)S(1)}, bf16[8,48,1024]{2,1,0:T(8,128)(2,1)S(1)}, u32[]{:S(2)}, u32[]{:S(2)}) %collective-permute-start.11) | collective-permute-done | bytes 786464 | tf_op jit(solution)/shard_map/ppermute | solution.py:478
  94.7 0.9 collective-permute-start.12
  95.5 1.0 collective-permute-done.14
  96.7 2.2 %collective-permute-start.15 = (bf16[4,48,1024]{2,1,0:T(8,128)(2,1)S(1)}, bf16[4,48,1024]{2,1,0:T(8,128)(2,1)S(1)}, u32[]{:S(2)}, u32[]{:S(2)}) collective-permute-start(bf16[4,48,1024]{2,1,0:T(8,128)(2,1)S(1)} %add_convert_fusion.1), channel_id=1, source_target_pairs={{0,4},{1,5},{2,6},{3,7},{4,0},{5,1},{6,2},{7,3},{8,12},{9,13},{10,... | collective-permute-start | bytes 1179656 | tf_op jit(solution)/shard_map/ppermute | solution.py:478
  99.0 0.8 collective-permute-start.18
  99.8 2.7 %collective-permute-done.12 = bf16[4,48,1024]{2,1,0:T(8,128)(2,1)S(1)} collective-permute-done((bf16[4,48,1024]{2,1,0:T(8,128)(2,1)S(1)}, bf16[4,48,1024]{2,1,0:T(8,128)(2,1)S(1)}, u32[]{:S(2)}, u32[]{:S(2)}) %collective-permute-start.12) | collective-permute-done | bytes 393248 | tf_op jit(solution)/shard_map/ppermute | solution.py:478
  102.6 0.8 collective-permute-start.13
  103.4 3.4 %collective-permute-done.15 = bf16[4,48,1024]{2,1,0:T(8,128)(2,1)S(1)} collective-permute-done((bf16[4,48,1024]{2,1,0:T(8,128)(2,1)S(1)}, bf16[4,48,1024]{2,1,0:T(8,128)(2,1)S(1)}, u32[]{:S(2)}, u32[]{:S(2)}) %collective-permute-start.15) | collective-permute-done | bytes 393248 | tf_op jit(solution)/shard_map/ppermute | solution.py:478
  106.9 1.4 %collective-permute-start.16 = (bf16[2,48,1024]{2,1,0:T(8,128)(2,1)S(1)}, bf16[2,48,1024]{2,1,0:T(8,128)(2,1)S(1)}, u32[]{:S(2)}, u32[]{:S(2)}) collective-permute-start(bf16[2,48,1024]{2,1,0:T(8,128)(2,1)S(1)} %add_convert_fusion.4), channel_id=1, source_target_pairs={{0,2},{1,3},{2,0},{3,1},{4,6},{5,7},{6,4},{7,5},{8,10},{9,11},{10,... | collective-permute-start | bytes 589832 | tf_op jit(solution)/shard_map/ppermute | solution.py:478
  108.3 1.5 %collective-permute-start.19 = (bf16[2,48,1024]{2,1,0:T(8,128)(2,1)S(1)}, bf16[2,48,1024]{2,1,0:T(8,128)(2,1)S(1)}, u32[]{:S(2)}, u32[]{:S(2)}) collective-permute-start(bf16[2,48,1024]{2,1,0:T(8,128)(2,1)S(1)} %add_convert_fusion.3), channel_id=1, source_target_pairs={{0,4},{1,5},{2,6},{3,7},{4,0},{5,1},{6,2},{7,3},{8,12},{9,13},{10,... | collective-permute-start | bytes 589832 | tf_op jit(solution)/shard_map/ppermute | solution.py:478
  110.0 2.7 %collective-permute-done.16 = bf16[2,48,1024]{2,1,0:T(8,128)(2,1)S(1)} collective-permute-done((bf16[2,48,1024]{2,1,0:T(8,128)(2,1)S(1)}, bf16[2,48,1024]{2,1,0:T(8,128)(2,1)S(1)}, u32[]{:S(2)}, u32[]{:S(2)}) %collective-permute-start.16) | collective-permute-done | bytes 196640 | tf_op jit(solution)/shard_map/ppermute | solution.py:478
  112.7 1.3 %collective-permute-done.19 = bf16[2,48,1024]{2,1,0:T(8,128)(2,1)S(1)} collective-permute-done((bf16[2,48,1024]{2,1,0:T(8,128)(2,1)S(1)}, bf16[2,48,1024]{2,1,0:T(8,128)(2,1)S(1)}, u32[]{:S(2)}, u32[]{:S(2)}) %collective-permute-start.19) | collective-permute-done | bytes 196640 | tf_op jit(solution)/shard_map/ppermute | solution.py:478
  114.2 3.4 %collective-permute-start.20 = (bf16[48,3072]{1,0:T(8,128)(2,1)S(1)}, bf16[48,3072]{1,0:T(8,128)(2,1)S(1)}, u32[]{:S(2)}, u32[]{:S(2)}) collective-permute-start(bf16[48,3072]{1,0:T(8,128)(2,1)S(1)} %pad_maximum_fusion.7), channel_id=1, source_target_pairs={{0,8},{1,9},{2,10},{3,11},{4,12},{5,13},{6,14},{7,15},{8,0},{9,1},... | collective-permute-start | bytes 884744 | tf_op jit(solution)/shard_map/ppermute | solution.py:478
  117.6 4.9 %shard_map.84 = bf16[512,768]{1,0:T(8,128)(2,1)} custom-call(f32[1,768]{1,0:T(1,128)S(1)} %copy-done.5, bf16[512,768]{1,0:T(8,128)(2,1)S(1)} %get-tuple-element.69.refs_1_, bf16[512,2304]{1,0:T(8,128)(2,1)S(1)} %get-tuple-element.70.refs_2_, bf16[512,768]{1,0:T(8,128)(2,1)S(1)} %bitcast.26, ...), custom_call_target="tpu_custom_call", output_to_operand_aliasing={{}: (10, {})} | custom-call | tf_op jit(solution)/shard_map/pallas_call | solution.py:383
  122.5 2.9 %collective-permute-done.20 = bf16[48,3072]{1,0:T(8,128)(2,1)S(1)} collective-permute-done((bf16[48,3072]{1,0:T(8,128)(2,1)S(1)}, bf16[48,3072]{1,0:T(8,128)(2,1)S(1)}, u32[]{:S(2)}, u32[]{:S(2)}) %collective-permute-start.20) | collective-permute-done | bytes 294944 | tf_op jit(solution)/shard_map/ppermute | solution.py:478
  125.4 0.9 fusion.1
  (37 shorter events, 1.7 us)
Async XLA Ops:
  0.6 16.5 %copy-start.5 = (f32[1,768]{1,0:T(1,128)S(1)}, f32[1,768]{1,0:T(1,128)}, u32[]{:S(2)}) copy-start(f32[1,768]{1,0:T(1,128)} %refs_0_.5) | copy-start | bytes 9220
  1.5 1.7 %copy-start = (bf16[1,1,512,2304]{3,2,1,0:T(8,128)(2,1)S(1)}, bf16[1,1,512,2304]{3,2,1,0:T(8,128)(2,1)}, u32[]{:S(2)}) copy-start(bf16[1,1,512,2304]{3,2,1,0:T(8,128)(2,1)} %param.7) | copy-start | bytes 7077892
  3.1 15.8 %copy-start.1 = (bf16[1,1,512,2304]{3,2,1,0:T(8,128)(2,1)S(1)}, bf16[1,1,512,2304]{3,2,1,0:T(8,128)(2,1)}, u32[]{:S(2)}) copy-start(bf16[1,1,512,2304]{3,2,1,0:T(8,128)(2,1)} %param.7) | copy-start | bytes 7077892
  13.0 12.3 %collective-permute-start = (bf16[1,48,3072]{2,1,0:T(8,128)(2,1)}, bf16[1,48,3072]{2,1,0:T(8,128)(2,1)S(1)}, u32[]{:S(2)}, u32[]{:S(2)}) collective-permute-start(bf16[1,48,3072]{2,1,0:T(8,128)(2,1)} %param.9), channel_id=1, source_target_pairs={{0,8},{1,9},{2,10},{3,11},{4,12},{5,13},{6,14},{7,15},{8,0},{9,1},... | collective-permute-start | bytes 884744 | tf_op jit(solution)/shard_map/ppermute | solution.py:478
  17.1 1.1 copy-start.2
  18.9 6.4 %copy-start.6 = (bf16[1,48,3072]{2,1,0:T(8,128)(2,1)S(1)}, bf16[1,48,3072]{2,1,0:T(8,128)(2,1)}, u32[]{:S(2)}) copy-start(bf16[1,48,3072]{2,1,0:T(8,128)(2,1)} %param.9) | copy-start | bytes 884740
  25.4 6.1 %collective-permute-start.5 = (bf16[2,48,1024]{2,1,0:T(8,128)(2,1)S(1)}, bf16[2,48,1024]{2,1,0:T(8,128)(2,1)S(1)}, u32[]{:S(2)}, u32[]{:S(2)}) collective-permute-start(bf16[2,48,1024]{2,1,0:T(8,128)(2,1)S(1)} %get-tuple-element.84), channel_id=1, source_target_pairs={{0,4},{1,5},{2,6},{3,7},{4,0},{5,1},{6,2},{7,3},{8,12},{9,13},{10,... | collective-permute-start | bytes 589832 | tf_op jit(solution)/shard_map/ppermute | solution.py:478
  26.5 6.8 %collective-permute-start.3 = (bf16[2,48,1024]{2,1,0:T(8,128)(2,1)S(1)}, bf16[2,48,1024]{2,1,0:T(8,128)(2,1)S(1)}, u32[]{:S(2)}, u32[]{:S(2)}) collective-permute-start(bf16[2,48,1024]{2,1,0:T(8,128)(2,1)S(1)} %get-tuple-element.85), channel_id=1, source_target_pairs={{0,2},{1,3},{2,0},{3,1},{4,6},{5,7},{6,4},{7,5},{8,10},{9,11},{10,... | collective-permute-start | bytes 589832 | tf_op jit(solution)/shard_map/ppermute | solution.py:478
  28.0 6.1 %collective-permute-start.1 = (bf16[2,48,1024]{2,1,0:T(8,128)(2,1)S(1)}, bf16[2,48,1024]{2,1,0:T(8,128)(2,1)S(1)}, u32[]{:S(2)}, u32[]{:S(2)}) collective-permute-start(bf16[2,48,1024]{2,1,0:T(8,128)(2,1)S(1)} %get-tuple-element.86), channel_id=1, source_target_pairs={{0,1},{1,0},{2,3},{3,2},{4,5},{5,4},{6,7},{7,6},{8,9},{9,8},{10,11... | collective-permute-start | bytes 589832 | tf_op jit(solution)/shard_map/ppermute | solution.py:478
  31.6 12.1 %collective-permute-start.6 = (bf16[4,48,1024]{2,1,0:T(8,128)(2,1)S(1)}, bf16[4,48,1024]{2,1,0:T(8,128)(2,1)S(1)}, u32[]{:S(2)}, u32[]{:S(2)}) collective-permute-start(bf16[4,48,1024]{2,1,0:T(8,128)(2,1)S(1)} %pad_maximum_fusion.6), channel_id=1, source_target_pairs={{0,1},{1,0},{2,3},{3,2},{4,5},{5,4},{6,7},{7,6},{8,9},{9,8},{10,11... | collective-permute-start | bytes 1179656 | tf_op jit(solution)/shard_map/ppermute | solution.py:478
  33.4 12.0 %collective-permute-start.4 = (bf16[4,48,1024]{2,1,0:T(8,128)(2,1)S(1)}, bf16[4,48,1024]{2,1,0:T(8,128)(2,1)S(1)}, u32[]{:S(2)}, u32[]{:S(2)}) collective-permute-start(bf16[4,48,1024]{2,1,0:T(8,128)(2,1)S(1)} %pad_maximum_fusion.5), channel_id=1, source_target_pairs={{0,4},{1,5},{2,6},{3,7},{4,0},{5,1},{6,2},{7,3},{8,12},{9,13},{10,... | collective-permute-start | bytes 1179656 | tf_op jit(solution)/shard_map/ppermute | solution.py:478
  34.2 12.1 %collective-permute-start.2 = (bf16[4,48,1024]{2,1,0:T(8,128)(2,1)S(1)}, bf16[4,48,1024]{2,1,0:T(8,128)(2,1)S(1)}, u32[]{:S(2)}, u32[]{:S(2)}) collective-permute-start(bf16[4,48,1024]{2,1,0:T(8,128)(2,1)S(1)} %pad_maximum_fusion.4), channel_id=1, source_target_pairs={{0,2},{1,3},{2,0},{3,1},{4,6},{5,7},{6,4},{7,5},{8,10},{9,11},{10,... | collective-permute-start | bytes 1179656 | tf_op jit(solution)/shard_map/ppermute | solution.py:478
  46.4 14.7 %copy-start.3 = (bf16[1,1,512,768]{3,2,1,0:T(8,128)(2,1)S(1)}, bf16[1,1,512,768]{3,2,1,0:T(8,128)(2,1)}, u32[]{:S(2)}) copy-start(bf16[1,1,512,768]{3,2,1,0:T(8,128)(2,1)} %param.6) | copy-start | bytes 2359300
  46.4 14.7 %copy-start.4 = (bf16[1,512,768]{2,1,0:T(8,128)(2,1)S(1)}, bf16[1,512,768]{2,1,0:T(8,128)(2,1)}, u32[]{:S(2)}) copy-start(bf16[1,512,768]{2,1,0:T(8,128)(2,1)} %param.11) | copy-start | bytes 2359300
  46.4 12.1 %collective-permute-start.7 = (bf16[8,48,1024]{2,1,0:T(8,128)(2,1)S(1)}, bf16[8,48,1024]{2,1,0:T(8,128)(2,1)S(1)}, u32[]{:S(2)}, u32[]{:S(2)}) collective-permute-start(bf16[8,48,1024]{2,1,0:T(8,128)(2,1)S(1)} %pad_maximum_fusion.refs_7_.refs_4_), channel_id=1, source_target_pairs={{0,4},{1,5},{2,6},{3,7},{4,0},{5,1},{6,2},{7,3},{8,12},{9,13},{10,... | collective-permute-start | bytes 2359304 | tf_op jit(solution)/shard_map/ppermute | solution.py:478
  47.9 12.0 %collective-permute-start.8 = (bf16[8,48,1024]{2,1,0:T(8,128)(2,1)S(1)}, bf16[8,48,1024]{2,1,0:T(8,128)(2,1)S(1)}, u32[]{:S(2)}, u32[]{:S(2)}) collective-permute-start(bf16[8,48,1024]{2,1,0:T(8,128)(2,1)S(1)} %pad_maximum_fusion.1.refs_9_.refs_6_), channel_id=1, source_target_pairs={{0,1},{1,0},{2,3},{3,2},{4,5},{5,4},{6,7},{7,6},{8,9},{9,8},{10,11... | collective-permute-start | bytes 2359304 | tf_op jit(solution)/shard_map/ppermute | solution.py:478
  49.2 12.0 %collective-permute-start.9 = (bf16[8,48,1024]{2,1,0:T(8,128)(2,1)S(1)}, bf16[8,48,1024]{2,1,0:T(8,128)(2,1)S(1)}, u32[]{:S(2)}, u32[]{:S(2)}) collective-permute-start(bf16[8,48,1024]{2,1,0:T(8,128)(2,1)S(1)} %pad_maximum_fusion.2.refs_11_.refs_8_), channel_id=1, source_target_pairs={{0,2},{1,3},{2,0},{3,1},{4,6},{5,7},{6,4},{7,5},{8,10},{9,11},{10,... | collective-permute-start | bytes 2359304 | tf_op jit(solution)/shard_map/ppermute | solution.py:478
  61.8 4.4 %collective-permute-start.10 = (bf16[512,768]{1,0:T(8,128)(2,1)}, bf16[512,768]{1,0:T(8,128)(2,1)S(1)}, u32[]{:S(2)}, u32[]{:S(2)}) collective-permute-start(bf16[512,768]{1,0:T(8,128)(2,1)} %get-tuple-element.66.refs_10_), channel_id=1, source_target_pairs={{16,0},{17,1},{18,2},{19,3},{20,4},{21,5},{22,6},{23,7},{24,8},{25... | collective-permute-start | bytes 2359304 | tf_op jit(solution)/shard_map/ppermute | solution.py:568
  78.3 16.3 %collective-permute-start.11 = (bf16[8,48,1024]{2,1,0:T(8,128)(2,1)S(1)}, bf16[8,48,1024]{2,1,0:T(8,128)(2,1)S(1)}, u32[]{:S(2)}, u32[]{:S(2)}) collective-permute-start(bf16[8,48,1024]{2,1,0:T(8,128)(2,1)S(1)} %get-tuple-element.73), channel_id=1, source_target_pairs={{0,4},{1,5},{2,6},{3,7},{4,0},{5,1},{6,2},{7,3},{8,12},{9,13},{10,... | collective-permute-start | bytes 2359304 | tf_op jit(solution)/shard_map/ppermute | solution.py:478
  79.0 17.6 %collective-permute-start.14 = (bf16[8,48,1024]{2,1,0:T(8,128)(2,1)S(1)}, bf16[8,48,1024]{2,1,0:T(8,128)(2,1)S(1)}, u32[]{:S(2)}, u32[]{:S(2)}) collective-permute-start(bf16[8,48,1024]{2,1,0:T(8,128)(2,1)S(1)} %get-tuple-element.75), channel_id=1, source_target_pairs={{0,1},{1,0},{2,3},{3,2},{4,5},{5,4},{6,7},{7,6},{8,9},{9,8},{10,11... | collective-permute-start | bytes 2359304 | tf_op jit(solution)/shard_map/ppermute | solution.py:478
  79.7 19.2 %collective-permute-start.17 = (bf16[8,48,1024]{2,1,0:T(8,128)(2,1)S(1)}, bf16[8,48,1024]{2,1,0:T(8,128)(2,1)S(1)}, u32[]{:S(2)}, u32[]{:S(2)}) collective-permute-start(bf16[8,48,1024]{2,1,0:T(8,128)(2,1)S(1)} %get-tuple-element.77), channel_id=1, source_target_pairs={{0,2},{1,3},{2,0},{3,1},{4,6},{5,7},{6,4},{7,5},{8,10},{9,11},{10,... | collective-permute-start | bytes 2359304 | tf_op jit(solution)/shard_map/ppermute | solution.py:478
  94.7 7.8 %collective-permute-start.12 = (bf16[4,48,1024]{2,1,0:T(8,128)(2,1)S(1)}, bf16[4,48,1024]{2,1,0:T(8,128)(2,1)S(1)}, u32[]{:S(2)}, u32[]{:S(2)}) collective-permute-start(bf16[4,48,1024]{2,1,0:T(8,128)(2,1)S(1)} %add_convert_fusion.2), channel_id=1, source_target_pairs={{0,2},{1,3},{2,0},{3,1},{4,6},{5,7},{6,4},{7,5},{8,10},{9,11},{10,... | collective-permute-start | bytes 1179656 | tf_op jit(solution)/shard_map/ppermute | solution.py:478
  96.7 10.1 %collective-permute-start.15 = (bf16[4,48,1024]{2,1,0:T(8,128)(2,1)S(1)}, bf16[4,48,1024]{2,1,0:T(8,128)(2,1)S(1)}, u32[]{:S(2)}, u32[]{:S(2)}) collective-permute-start(bf16[4,48,1024]{2,1,0:T(8,128)(2,1)S(1)} %add_convert_fusion.1), channel_id=1, source_target_pairs={{0,4},{1,5},{2,6},{3,7},{4,0},{5,1},{6,2},{7,3},{8,12},{9,13},{10,... | collective-permute-start | bytes 1179656 | tf_op jit(solution)/shard_map/ppermute | solution.py:478
  99.0 9.2 %collective-permute-start.18 = (bf16[4,48,1024]{2,1,0:T(8,128)(2,1)S(1)}, bf16[4,48,1024]{2,1,0:T(8,128)(2,1)S(1)}, u32[]{:S(2)}, u32[]{:S(2)}) collective-permute-start(bf16[4,48,1024]{2,1,0:T(8,128)(2,1)S(1)} %add_convert_fusion), channel_id=1, source_target_pairs={{0,1},{1,0},{2,3},{3,2},{4,5},{5,4},{6,7},{7,6},{8,9},{9,8},{10,11... | collective-permute-start | bytes 1179656 | tf_op jit(solution)/shard_map/ppermute | solution.py:478
  102.6 7.2 %collective-permute-start.13 = (bf16[2,48,1024]{2,1,0:T(8,128)(2,1)S(1)}, bf16[2,48,1024]{2,1,0:T(8,128)(2,1)S(1)}, u32[]{:S(2)}, u32[]{:S(2)}) collective-permute-start(bf16[2,48,1024]{2,1,0:T(8,128)(2,1)S(1)} %add_convert_fusion.5), channel_id=1, source_target_pairs={{0,1},{1,0},{2,3},{3,2},{4,5},{5,4},{6,7},{7,6},{8,9},{9,8},{10,11... | collective-permute-start | bytes 589832 | tf_op jit(solution)/shard_map/ppermute | solution.py:478
  106.9 5.7 %collective-permute-start.16 = (bf16[2,48,1024]{2,1,0:T(8,128)(2,1)S(1)}, bf16[2,48,1024]{2,1,0:T(8,128)(2,1)S(1)}, u32[]{:S(2)}, u32[]{:S(2)}) collective-permute-start(bf16[2,48,1024]{2,1,0:T(8,128)(2,1)S(1)} %add_convert_fusion.4), channel_id=1, source_target_pairs={{0,2},{1,3},{2,0},{3,1},{4,6},{5,7},{6,4},{7,5},{8,10},{9,11},{10,... | collective-permute-start | bytes 589832 | tf_op jit(solution)/shard_map/ppermute | solution.py:478
  108.3 5.7 %collective-permute-start.19 = (bf16[2,48,1024]{2,1,0:T(8,128)(2,1)S(1)}, bf16[2,48,1024]{2,1,0:T(8,128)(2,1)S(1)}, u32[]{:S(2)}, u32[]{:S(2)}) collective-permute-start(bf16[2,48,1024]{2,1,0:T(8,128)(2,1)S(1)} %add_convert_fusion.3), channel_id=1, source_target_pairs={{0,4},{1,5},{2,6},{3,7},{4,0},{5,1},{6,2},{7,3},{8,12},{9,13},{10,... | collective-permute-start | bytes 589832 | tf_op jit(solution)/shard_map/ppermute | solution.py:478
  114.2 11.2 %collective-permute-start.20 = (bf16[48,3072]{1,0:T(8,128)(2,1)S(1)}, bf16[48,3072]{1,0:T(8,128)(2,1)S(1)}, u32[]{:S(2)}, u32[]{:S(2)}) collective-permute-start(bf16[48,3072]{1,0:T(8,128)(2,1)S(1)} %pad_maximum_fusion.7), channel_id=1, source_target_pairs={{0,8},{1,9},{2,10},{3,11},{4,12},{5,13},{6,14},{7,15},{8,0},{9,1},... | collective-permute-start | bytes 884744 | tf_op jit(solution)/shard_map/ppermute | solution.py:478
where the time goes:
time: 127 us; the launch traced here: 126 us
  waiting for transfers between devices  61 us (48%)
  starting transfers between devices  30 us (24%)
  Pallas kernels  28.4 us (22%)
  local copies, waits for them, and re-layouts  3.7 us (3%)
  other arithmetic  2.29 us (2%)
    ppermute x20, waiting for transfers between devices, across(): lax.ppermute(value, 'dp', [(source, source ^ bit) for source in range(cou...  57.9 us
    ppermute x20, starting transfers between devices, across(): lax.ppermute(value, 'dp', [(source, source ^ bit) for source in range(cou...  28.7 us
    pallas_call x4, Pallas kernels, forward(): call(body, (shape((HEADS, length, length)), shape((length, INNER)), shape...  10.1 us
    pallas_call x2, Pallas kernels, section_backward(): call(body, tuple(outs), specs + [ANY] * (len(inputs) - len(specs)), (ANY,...  10.1 us
    pallas_call x1, Pallas kernels, project(): call(body, shape((length, width)), [VMEM] * 3 + [ANY] * (len(inputs) - 3)...  4.94 us
    unnamed x15, local copies, waits for them, and re-layouts  3.66 us
    ppermute x1, waiting for transfers between devices, on_device(): lax.ppermute(carry[2], 'pipe', [(source, source - 1) for source in range(...  3.09 us
    pallas_call x1, Pallas kernels, weight_terms(): call(body, outs, [VMEM] * len(inputs), (VMEM,) * len(outs), [pltpu.VMEM((...  2.62 us
  transfers between devices with their start and end apart: 21, of which 17 were waited for; matrix products, arithmetic and copies ran while one was open for 1% of the time, Pallas kernels for 5%

commit v1 on v0

--- a/solution.py
+++ b/solution.py
@@ -512,8 +512,6 @@
     kept = [[terms[2 * c]] for c in range(chunk_count)]
     outgoing = [terms[2 * c + 1] for c in range(chunk_count)]
     for step in reversed(range(steps)):
-        if step == 0 and all(order[0] == orders[0][0] for order in orders):
-            break
         got = [across(outgoing[c], orders[c][step]) for c in range(chunk_count)]
         for c in range(chunk_count):
             kept[c].append(got[c])
@@ -540,7 +538,8 @@
 
     orders = bit_orders(replicas, 3)
     gather = Gather(shard, orders)
-    saved = forward((0, PAIRS), rand, qkv, None)
+    early = pltpu.with_memory_space_constraint(qkv, pltpu.HBM)
+    saved = forward((0, PAIRS), rand, early, None)
     saved = gather.after(*saved)
     gather.advance()
     share = PAIRS // 3

time: 127 us -> 123 us (0.969)
  waiting for transfers between devices: 61 us -> 54.2 us
  starting transfers between devices: 30 us -> 33.2 us
  local copies, waits for them, and re-layouts: 3.7 us -> 2.19 us
  Pallas kernels: 28.4 us -> 29.9 us
    ppermute x20 -> x22, waiting for transfers between devices: 57.9 us -> 51.1 us  [across(): lax.ppermute(value, 'dp', [(source, source ^ bit) for source in range(cou...]
    ppermute x20 -> x22, starting transfers between devices: 28.7 us -> 31.9 us  [across(): lax.ppermute(value, 'dp', [(source, source ^ bit) for source in range(cou...]
    unnamed x15 -> x13, local copies, waits for them, and re-layouts: 3.66 us -> 2.14 us
    pallas_call x4, Pallas kernels: 10.1 us -> 11.6 us  [forward(): call(body, (shape((HEADS, length, length)), shape((length, INNER)), shape...]
  transfers between devices with their start and end apart: 21 -> 23, of which waited for: 17 -> 16; matrix products, arithmetic and copies ran while one was open for 1% -> 1% of each run, Pallas kernels for 5% -> 5%
where the time goes in v1:
time: 123 us
  waiting for transfers between devices  54.2 us (44%)
  starting transfers between devices  33.2 us (27%)
  Pallas kernels  29.9 us (24%)
  other arithmetic  2.26 us (2%)
  local copies, waits for them, and re-layouts  2.19 us (2%)
    ppermute x22, waiting for transfers between devices, across(): lax.ppermute(value, 'dp', [(source, source ^ bit) for source in range(cou...  51.1 us
    ppermute x22, starting transfers between devices, across(): lax.ppermute(value, 'dp', [(source, source ^ bit) for source in range(cou...  31.9 us
    pallas_call x4, Pallas kernels, forward(): call(body, (shape((HEADS, length, length)), shape((length, INNER)), shape...  11.6 us
    pallas_call x2, Pallas kernels, section_backward(): call(body, tuple(outs), specs + [ANY] * (len(inputs) - len(specs)), (ANY,...  10 us
    pallas_call x1, Pallas kernels, project(): call(body, shape((length, width)), [VMEM] * 3 + [ANY] * (len(inputs) - 3)...  4.97 us
    ppermute x1, waiting for transfers between devices, on_device(): lax.ppermute(carry[2], 'pipe', [(source, source - 1) for source in range(...  3.09 us
    pallas_call x1, Pallas kernels, weight_terms(): call(body, outs, [VMEM] * len(inputs), (VMEM,) * len(outs), [pltpu.VMEM((...  2.61 us
  transfers between devices with their start and end apart: 23, of which 16 were waited for; matrix products, arithmetic and copies ran while one was open for 1% of the time, Pallas kernels for 5%

profile of v1, /device:TPU:0, one launch (start us, length us, event | category | flops | bytes accessed | tf_op | source)
XLA Modules:
  0.0 122.6 jit_solution(106880978816458800)
XLA Ops:
  0.7 1.0 copy.20
  1.6 11.3 %shard_map.77 = (bf16[12,512,512]{2,1,0:T(8,128)(2,1)S(1)}, bf16[512,768]{1,0:T(8,128)(2,1)S(1)}, bf16[512,2304]{1,0:T(8,128)(2,1)S(1)}) custom-call(s32[12,6,3]{2,1,0:T(8,128)S(1)} %bitcast.16, bf16[512,2304]{1,0:T(8,128)(2,1)} %bitcast.5), custom_call_target="tpu_custom_call" | custom-call | tf_op jit(solution)/shard_map/pallas_call | solution.py:167
  13.0 4.1 %collective-permute-start = (bf16[1,48,3072]{2,1,0:T(8,128)(2,1)}, bf16[1,48,3072]{2,1,0:T(8,128)(2,1)S(1)}, u32[]{:S(2)}, u32[]{:S(2)}) collective-permute-start(bf16[1,48,3072]{2,1,0:T(8,128)(2,1)} %param.9), channel_id=1, source_target_pairs={{0,8},{1,9},{2,10},{3,11},{4,12},{5,13},{6,14},{7,15},{8,0},{9,1},... | collective-permute-start | bytes 884744 | tf_op jit(solution)/shard_map/ppermute | solution.py:478
  17.1 1.1 copy-done.1
  18.2 0.7 shard_map.79.refs_0_
  19.0 6.3 %collective-permute-done = bf16[1,48,3072]{2,1,0:T(8,128)(2,1)S(1)} collective-permute-done((bf16[1,48,3072]{2,1,0:T(8,128)(2,1)}, bf16[1,48,3072]{2,1,0:T(8,128)(2,1)S(1)}, u32[]{:S(2)}, u32[]{:S(2)}) %collective-permute-start) | collective-permute-done | bytes 294944 | tf_op jit(solution)/shard_map/ppermute | solution.py:478
  25.4 1.1 collective-permute-start.5
  26.5 1.5 %collective-permute-start.3 = (bf16[2,48,1024]{2,1,0:T(8,128)(2,1)S(1)}, bf16[2,48,1024]{2,1,0:T(8,128)(2,1)S(1)}, u32[]{:S(2)}, u32[]{:S(2)}) collective-permute-start(bf16[2,48,1024]{2,1,0:T(8,128)(2,1)S(1)} %get-tuple-element.79), channel_id=1, source_target_pairs={{0,2},{1,3},{2,0},{3,1},{4,6},{5,7},{6,4},{7,5},{8,10},{9,11},{10,... | collective-permute-start | bytes 589832 | tf_op jit(solution)/shard_map/ppermute | solution.py:478
  28.0 1.5 %collective-permute-start.1 = (bf16[2,48,1024]{2,1,0:T(8,128)(2,1)S(1)}, bf16[2,48,1024]{2,1,0:T(8,128)(2,1)S(1)}, u32[]{:S(2)}, u32[]{:S(2)}) collective-permute-start(bf16[2,48,1024]{2,1,0:T(8,128)(2,1)S(1)} %get-tuple-element.80), channel_id=1, source_target_pairs={{0,1},{1,0},{2,3},{3,2},{4,5},{5,4},{6,7},{7,6},{8,9},{9,8},{10,11... | collective-permute-start | bytes 589832 | tf_op jit(solution)/shard_map/ppermute | solution.py:478
  29.5 2.4 %collective-permute-done.5 = bf16[2,48,1024]{2,1,0:T(8,128)(2,1)S(1)} collective-permute-done((bf16[2,48,1024]{2,1,0:T(8,128)(2,1)S(1)}, bf16[2,48,1024]{2,1,0:T(8,128)(2,1)S(1)}, u32[]{:S(2)}, u32[]{:S(2)}) %collective-permute-start.5) | collective-permute-done | bytes 196640 | tf_op jit(solution)/shard_map/ppermute | solution.py:478
  31.9 2.5 %collective-permute-start.6 = (bf16[4,48,1024]{2,1,0:T(8,128)(2,1)S(1)}, bf16[4,48,1024]{2,1,0:T(8,128)(2,1)S(1)}, u32[]{:S(2)}, u32[]{:S(2)}) collective-permute-start(bf16[4,48,1024]{2,1,0:T(8,128)(2,1)S(1)} %pad_maximum_fusion.6), channel_id=1, source_target_pairs={{0,1},{1,0},{2,3},{3,2},{4,5},{5,4},{6,7},{7,6},{8,9},{9,8},{10,11... | collective-permute-start | bytes 1179656 | tf_op jit(solution)/shard_map/ppermute | solution.py:478
  34.4 0.7 collective-permute-start.4
  35.1 0.6 collective-permute-done.1
  35.8 0.9 collective-permute-start.2
  36.8 7.6 %collective-permute-done.6 = bf16[4,48,1024]{2,1,0:T(8,128)(2,1)S(1)} collective-permute-done((bf16[4,48,1024]{2,1,0:T(8,128)(2,1)S(1)}, bf16[4,48,1024]{2,1,0:T(8,128)(2,1)S(1)}, u32[]{:S(2)}, u32[]{:S(2)}) %collective-permute-start.6) | collective-permute-done | bytes 393248 | tf_op jit(solution)/shard_map/ppermute | solution.py:478
  44.6 0.2 collective-permute-done.2
  44.9 1.1 collective-permute-start.7
  45.9 1.8 %collective-permute-start.8 = (bf16[8,48,1024]{2,1,0:T(8,128)(2,1)S(1)}, bf16[8,48,1024]{2,1,0:T(8,128)(2,1)S(1)}, u32[]{:S(2)}, u32[]{:S(2)}) collective-permute-start(bf16[8,48,1024]{2,1,0:T(8,128)(2,1)S(1)} %pad_maximum_fusion.1.refs_9_.refs_6_), channel_id=1, source_target_pairs={{0,1},{1,0},{2,3},{3,2},{4,5},{5,4},{6,7},{7,6},{8,9},{9,8},{10,11... | collective-permute-start | bytes 2359304 | tf_op jit(solution)/shard_map/ppermute | solution.py:478
  47.7 1.5 %collective-permute-start.9 = (bf16[8,48,1024]{2,1,0:T(8,128)(2,1)S(1)}, bf16[8,48,1024]{2,1,0:T(8,128)(2,1)S(1)}, u32[]{:S(2)}, u32[]{:S(2)}) collective-permute-start(bf16[8,48,1024]{2,1,0:T(8,128)(2,1)S(1)} %pad_maximum_fusion.2.refs_11_.refs_8_), channel_id=1, source_target_pairs={{0,2},{1,3},{2,0},{3,1},{4,6},{5,7},{6,4},{7,5},{8,10},{9,11},{10,... | collective-permute-start | bytes 2359304 | tf_op jit(solution)/shard_map/ppermute | solution.py:478
  49.4 7.6 %collective-permute-done.7.refs_8_.refs_5_ = bf16[8,48,1024]{2,1,0:T(8,128)(2,1)S(1)} collective-permute-done((bf16[8,48,1024]{2,1,0:T(8,128)(2,1)S(1)}, bf16[8,48,1024]{2,1,0:T(8,128)(2,1)S(1)}, u32[]{:S(2)}, u32[]{:S(2)}) %collective-permute-start.7) | collective-permute-done | bytes 786464 | tf_op jit(solution)/shard_map/ppermute | solution.py:478
  56.9 1.0 collective-permute-done.8.refs_10_.refs_7_
  57.9 1.8 %collective-permute-done.9.refs_12_.refs_9_ = bf16[8,48,1024]{2,1,0:T(8,128)(2,1)S(1)} collective-permute-done((bf16[8,48,1024]{2,1,0:T(8,128)(2,1)S(1)}, bf16[8,48,1024]{2,1,0:T(8,128)(2,1)S(1)}, u32[]{:S(2)}, u32[]{:S(2)}) %collective-permute-start.9) | collective-permute-done | bytes 786464 | tf_op jit(solution)/shard_map/ppermute | solution.py:478
  59.7 0.6 shard_map.82
  60.4 1.3 %collective-permute-start.10 = (bf16[512,768]{1,0:T(8,128)(2,1)}, bf16[512,768]{1,0:T(8,128)(2,1)S(1)}, u32[]{:S(2)}, u32[]{:S(2)}) collective-permute-start(bf16[512,768]{1,0:T(8,128)(2,1)} %get-tuple-element.66.refs_10_), channel_id=1, source_target_pairs={{16,0},{17,1},{18,2},{19,3},{20,4},{21,5},{22,6},{23,7},{24,8},{25... | collective-permute-start | bytes 2359304 | tf_op jit(solution)/shard_map/ppermute | solution.py:567
  61.7 3.1 %collective-permute-done.10.refs_1_ = bf16[512,768]{1,0:T(8,128)(2,1)S(1)} collective-permute-done((bf16[512,768]{1,0:T(8,128)(2,1)}, bf16[512,768]{1,0:T(8,128)(2,1)S(1)}, u32[]{:S(2)}, u32[]{:S(2)}) %collective-permute-start.10) | collective-permute-done | bytes 786464 | tf_op jit(solution)/shard_map/ppermute | solution.py:567
  64.8 9.4 %shard_map.83 = (bf16[512,768]{1,0:T(8,128)(2,1)S(1)}, bf16[512,2304]{1,0:T(8,128)(2,1)S(1)}) custom-call(f32[1,768]{1,0:T(1,128)S(1)} %copy-done.4, bf16[512,768]{1,0:T(8,128)(2,1)S(1)} %collective-permute-done.10.refs_1_, bf16[512,768]{1,0:T(8,128)(2,1)S(1)} %bitcast.15, ...), custom_call_target="tpu_custom_call", output_to_operand_aliasing={{0}: (13, {}), {1}: (14, {})} | custom-call | tf_op jit(solution)/shard_map/pallas_call | solution.py:352
  74.2 2.6 %shard_map.85 = (bf16[8,48,1024]{2,1,0:T(8,128)(2,1)S(1)}, bf16[8,48,1024]{2,1,0:T(8,128)(2,1)S(1)}, bf16[8,48,1024]{2,1,0:T(8,128)(2,1)S(1)}, bf16[8,48,1024]{2...) custom-call(bf16[768,512]{1,0:T(8,128)(2,1)S(1)} %shard_map.79.refs_0_, ...), custom_call_target="tpu_custom_call" | custom-call | tf_op jit(solution)/shard_map/pallas_call | solution.py:443
  76.8 1.1 collective-permute-start.11
  77.9 0.3 collective-permute-start.15
  78.2 1.5 %collective-permute-start.19 = (bf16[8,48,1024]{2,1,0:T(8,128)(2,1)S(1)}, bf16[8,48,1024]{2,1,0:T(8,128)(2,1)S(1)}, u32[]{:S(2)}, u32[]{:S(2)}) collective-permute-start(bf16[8,48,1024]{2,1,0:T(8,128)(2,1)S(1)} %get-tuple-element.77), channel_id=1, source_target_pairs={{0,2},{1,3},{2,0},{3,1},{4,6},{5,7},{6,4},{7,5},{8,10},{9,11},{10,... | collective-permute-start | bytes 2359304 | tf_op jit(solution)/shard_map/ppermute | solution.py:478
  79.7 5.0 %shard_map.84 = bf16[512,768]{1,0:T(8,128)(2,1)} custom-call(f32[1,768]{1,0:T(1,128)S(1)} %copy-done.4, bf16[512,768]{1,0:T(8,128)(2,1)S(1)} %get-tuple-element.69.refs_1_, bf16[512,2304]{1,0:T(8,128)(2,1)S(1)} %get-tuple-element.70.refs_2_, bf16[512,768]{1,0:T(8,128)(2,1)S(1)} %bitcast.12, ...), custom_call_target="tpu_custom_call", output_to_operand_aliasing={{}: (10, {})} | custom-call | tf_op jit(solution)/shard_map/pallas_call | solution.py:383
  84.7 8.4 %collective-permute-done.11 = bf16[8,48,1024]{2,1,0:T(8,128)(2,1)S(1)} collective-permute-done((bf16[8,48,1024]{2,1,0:T(8,128)(2,1)S(1)}, bf16[8,48,1024]{2,1,0:T(8,128)(2,1)S(1)}, u32[]{:S(2)}, u32[]{:S(2)}) %collective-permute-start.11) | collective-permute-done | bytes 786464 | tf_op jit(solution)/shard_map/ppermute | solution.py:478
  93.2 1.6 %collective-permute-start.12 = (bf16[4,48,1024]{2,1,0:T(8,128)(2,1)S(1)}, bf16[4,48,1024]{2,1,0:T(8,128)(2,1)S(1)}, u32[]{:S(2)}, u32[]{:S(2)}) collective-permute-start(bf16[4,48,1024]{2,1,0:T(8,128)(2,1)S(1)} %add_convert_fusion.2), channel_id=1, source_target_pairs={{0,2},{1,3},{2,0},{3,1},{4,6},{5,7},{6,4},{7,5},{8,10},{9,11},{10,... | collective-permute-start | bytes 1179656 | tf_op jit(solution)/shard_map/ppermute | solution.py:478
  94.8 1.0 collective-permute-done.15
  95.9 0.8 collective-permute-start.16
  96.9 0.2 collective-permute-start.20
  97.1 3.9 %collective-permute-done.12 = bf16[4,48,1024]{2,1,0:T(8,128)(2,1)S(1)} collective-permute-done((bf16[4,48,1024]{2,1,0:T(8,128)(2,1)S(1)}, bf16[4,48,1024]{2,1,0:T(8,128)(2,1)S(1)}, u32[]{:S(2)}, u32[]{:S(2)}) %collective-permute-start.12) | collective-permute-done | bytes 393248 | tf_op jit(solution)/shard_map/ppermute | solution.py:478
  101.1 0.3 collective-permute-start.13
  101.4 5.5 %collective-permute-done.16 = bf16[4,48,1024]{2,1,0:T(8,128)(2,1)S(1)} collective-permute-done((bf16[4,48,1024]{2,1,0:T(8,128)(2,1)S(1)}, bf16[4,48,1024]{2,1,0:T(8,128)(2,1)S(1)}, u32[]{:S(2)}, u32[]{:S(2)}) %collective-permute-start.16) | collective-permute-done | bytes 393248 | tf_op jit(solution)/shard_map/ppermute | solution.py:478
  107.0 1.6 %collective-permute-start.17 = (bf16[2,48,1024]{2,1,0:T(8,128)(2,1)S(1)}, bf16[2,48,1024]{2,1,0:T(8,128)(2,1)S(1)}, u32[]{:S(2)}, u32[]{:S(2)}) collective-permute-start(bf16[2,48,1024]{2,1,0:T(8,128)(2,1)S(1)} %add_convert_fusion.4), channel_id=1, source_target_pairs={{0,2},{1,3},{2,0},{3,1},{4,6},{5,7},{6,4},{7,5},{8,10},{9,11},{10,... | collective-permute-start | bytes 589832 | tf_op jit(solution)/shard_map/ppermute | solution.py:478
  108.7 1.1 collective-permute-start.21
  109.8 2.6 %collective-permute-start.14 = (bf16[1,48,1024]{2,1,0:T(8,128)(2,1)S(1)}, bf16[1,48,1024]{2,1,0:T(8,128)(2,1)S(1)}, u32[]{:S(2)}, u32[]{:S(2)}) collective-permute-start(bf16[1,48,1024]{2,1,0:T(8,128)(2,1)S(1)} %add_convert_fusion.8), channel_id=1, source_target_pairs={{0,8},{1,9},{2,10},{3,11},{4,12},{5,13},{6,14},{7,15},{8,0},{9,1},... | collective-permute-start | bytes 294920 | tf_op jit(solution)/shard_map/ppermute | solution.py:478
  112.4 0.3 collective-permute-done.17
  112.8 2.2 %collective-permute-start.18 = (bf16[1,48,1024]{2,1,0:T(8,128)(2,1)S(1)}, bf16[1,48,1024]{2,1,0:T(8,128)(2,1)S(1)}, u32[]{:S(2)}, u32[]{:S(2)}) collective-permute-start(bf16[1,48,1024]{2,1,0:T(8,128)(2,1)S(1)} %add_convert_fusion.7), channel_id=1, source_target_pairs={{0,8},{1,9},{2,10},{3,11},{4,12},{5,13},{6,14},{7,15},{8,0},{9,1},... | collective-permute-start | bytes 294920 | tf_op jit(solution)/shard_map/ppermute | solution.py:478
  115.0 1.9 %collective-permute-start.22 = (bf16[1,48,1024]{2,1,0:T(8,128)(2,1)S(1)}, bf16[1,48,1024]{2,1,0:T(8,128)(2,1)S(1)}, u32[]{:S(2)}, u32[]{:S(2)}) collective-permute-start(bf16[1,48,1024]{2,1,0:T(8,128)(2,1)S(1)} %add_convert_fusion.6), channel_id=1, source_target_pairs={{0,8},{1,9},{2,10},{3,11},{4,12},{5,13},{6,14},{7,15},{8,0},{9,1},... | collective-permute-start | bytes 294920 | tf_op jit(solution)/shard_map/ppermute | solution.py:478
  117.0 2.4 %collective-permute-done.18 = bf16[1,48,1024]{2,1,0:T(8,128)(2,1)S(1)} collective-permute-done((bf16[1,48,1024]{2,1,0:T(8,128)(2,1)S(1)}, bf16[1,48,1024]{2,1,0:T(8,128)(2,1)S(1)}, u32[]{:S(2)}, u32[]{:S(2)}) %collective-permute-start.18) | collective-permute-done | bytes 98336 | tf_op jit(solution)/shard_map/ppermute | solution.py:478
  119.5 2.2 %collective-permute-done.22 = bf16[1,48,1024]{2,1,0:T(8,128)(2,1)S(1)} collective-permute-done((bf16[1,48,1024]{2,1,0:T(8,128)(2,1)S(1)}, bf16[1,48,1024]{2,1,0:T(8,128)(2,1)S(1)}, u32[]{:S(2)}, u32[]{:S(2)}) %collective-permute-start.22) | collective-permute-done | bytes 98336 | tf_op jit(solution)/shard_map/ppermute | solution.py:478
  121.7 0.9 maximum_multiply_fusion
  (41 shorter events, 1.8 us)
Async XLA Ops:
  0.6 18.2 %copy-start = (bf16[1,1,512,2304]{3,2,1,0:T(8,128)(2,1)S(1)}, bf16[1,1,512,2304]{3,2,1,0:T(8,128)(2,1)}, u32[]{:S(2)}) copy-start(bf16[1,1,512,2304]{3,2,1,0:T(8,128)(2,1)} %param.7) | copy-start | bytes 7077892
  0.6 16.4 %copy-start.4 = (f32[1,768]{1,0:T(1,128)S(1)}, f32[1,768]{1,0:T(1,128)}, u32[]{:S(2)}) copy-start(f32[1,768]{1,0:T(1,128)} %refs_0_.5) | copy-start | bytes 9220
  13.0 12.3 %collective-permute-start = (bf16[1,48,3072]{2,1,0:T(8,128)(2,1)}, bf16[1,48,3072]{2,1,0:T(8,128)(2,1)S(1)}, u32[]{:S(2)}, u32[]{:S(2)}) collective-permute-start(bf16[1,48,3072]{2,1,0:T(8,128)(2,1)} %param.9), channel_id=1, source_target_pairs={{0,8},{1,9},{2,10},{3,11},{4,12},{5,13},{6,14},{7,15},{8,0},{9,1},... | collective-permute-start | bytes 884744 | tf_op jit(solution)/shard_map/ppermute | solution.py:478
  17.1 1.1 copy-start.1
  18.9 6.4 %copy-start.5 = (bf16[1,48,3072]{2,1,0:T(8,128)(2,1)S(1)}, bf16[1,48,3072]{2,1,0:T(8,128)(2,1)}, u32[]{:S(2)}) copy-start(bf16[1,48,3072]{2,1,0:T(8,128)(2,1)} %param.9) | copy-start | bytes 884740
  25.4 6.5 %collective-permute-start.5 = (bf16[2,48,1024]{2,1,0:T(8,128)(2,1)S(1)}, bf16[2,48,1024]{2,1,0:T(8,128)(2,1)S(1)}, u32[]{:S(2)}, u32[]{:S(2)}) collective-permute-start(bf16[2,48,1024]{2,1,0:T(8,128)(2,1)S(1)} %get-tuple-element.78), channel_id=1, source_target_pairs={{0,4},{1,5},{2,6},{3,7},{4,0},{5,1},{6,2},{7,3},{8,12},{9,13},{10,... | collective-permute-start | bytes 589832 | tf_op jit(solution)/shard_map/ppermute | solution.py:478
  26.5 7.9 %collective-permute-start.3 = (bf16[2,48,1024]{2,1,0:T(8,128)(2,1)S(1)}, bf16[2,48,1024]{2,1,0:T(8,128)(2,1)S(1)}, u32[]{:S(2)}, u32[]{:S(2)}) collective-permute-start(bf16[2,48,1024]{2,1,0:T(8,128)(2,1)S(1)} %get-tuple-element.79), channel_id=1, source_target_pairs={{0,2},{1,3},{2,0},{3,1},{4,6},{5,7},{6,4},{7,5},{8,10},{9,11},{10,... | collective-permute-start | bytes 589832 | tf_op jit(solution)/shard_map/ppermute | solution.py:478
  28.0 7.8 %collective-permute-start.1 = (bf16[2,48,1024]{2,1,0:T(8,128)(2,1)S(1)}, bf16[2,48,1024]{2,1,0:T(8,128)(2,1)S(1)}, u32[]{:S(2)}, u32[]{:S(2)}) collective-permute-start(bf16[2,48,1024]{2,1,0:T(8,128)(2,1)S(1)} %get-tuple-element.80), channel_id=1, source_target_pairs={{0,1},{1,0},{2,3},{3,2},{4,5},{5,4},{6,7},{7,6},{8,9},{9,8},{10,11... | collective-permute-start | bytes 589832 | tf_op jit(solution)/shard_map/ppermute | solution.py:478
  31.9 12.5 %collective-permute-start.6 = (bf16[4,48,1024]{2,1,0:T(8,128)(2,1)S(1)}, bf16[4,48,1024]{2,1,0:T(8,128)(2,1)S(1)}, u32[]{:S(2)}, u32[]{:S(2)}) collective-permute-start(bf16[4,48,1024]{2,1,0:T(8,128)(2,1)S(1)} %pad_maximum_fusion.6), channel_id=1, source_target_pairs={{0,1},{1,0},{2,3},{3,2},{4,5},{5,4},{6,7},{7,6},{8,9},{9,8},{10,11... | collective-permute-start | bytes 1179656 | tf_op jit(solution)/shard_map/ppermute | solution.py:478
  34.4 10.1 %collective-permute-start.4 = (bf16[4,48,1024]{2,1,0:T(8,128)(2,1)S(1)}, bf16[4,48,1024]{2,1,0:T(8,128)(2,1)S(1)}, u32[]{:S(2)}, u32[]{:S(2)}) collective-permute-start(bf16[4,48,1024]{2,1,0:T(8,128)(2,1)S(1)} %pad_maximum_fusion.5), channel_id=1, source_target_pairs={{0,4},{1,5},{2,6},{3,7},{4,0},{5,1},{6,2},{7,3},{8,12},{9,13},{10,... | collective-permute-start | bytes 1179656 | tf_op jit(solution)/shard_map/ppermute | solution.py:478
  35.8 9.0 %collective-permute-start.2 = (bf16[4,48,1024]{2,1,0:T(8,128)(2,1)S(1)}, bf16[4,48,1024]{2,1,0:T(8,128)(2,1)S(1)}, u32[]{:S(2)}, u32[]{:S(2)}) collective-permute-start(bf16[4,48,1024]{2,1,0:T(8,128)(2,1)S(1)} %pad_maximum_fusion.4), channel_id=1, source_target_pairs={{0,2},{1,3},{2,0},{3,1},{4,6},{5,7},{6,4},{7,5},{8,10},{9,11},{10,... | collective-permute-start | bytes 1179656 | tf_op jit(solution)/shard_map/ppermute | solution.py:478
  44.9 14.9 %copy-start.2 = (bf16[1,1,512,768]{3,2,1,0:T(8,128)(2,1)S(1)}, bf16[1,1,512,768]{3,2,1,0:T(8,128)(2,1)}, u32[]{:S(2)}) copy-start(bf16[1,1,512,768]{3,2,1,0:T(8,128)(2,1)} %param.6) | copy-start | bytes 2359300
  44.9 14.9 %copy-start.3 = (bf16[1,512,768]{2,1,0:T(8,128)(2,1)S(1)}, bf16[1,512,768]{2,1,0:T(8,128)(2,1)}, u32[]{:S(2)}) copy-start(bf16[1,512,768]{2,1,0:T(8,128)(2,1)} %param.11) | copy-start | bytes 2359300
  44.9 12.1 %collective-permute-start.7 = (bf16[8,48,1024]{2,1,0:T(8,128)(2,1)S(1)}, bf16[8,48,1024]{2,1,0:T(8,128)(2,1)S(1)}, u32[]{:S(2)}, u32[]{:S(2)}) collective-permute-start(bf16[8,48,1024]{2,1,0:T(8,128)(2,1)S(1)} %pad_maximum_fusion.refs_7_.refs_4_), channel_id=1, source_target_pairs={{0,4},{1,5},{2,6},{3,7},{4,0},{5,1},{6,2},{7,3},{8,12},{9,13},{10,... | collective-permute-start | bytes 2359304 | tf_op jit(solution)/shard_map/ppermute | solution.py:478
  45.9 12.0 %collective-permute-start.8 = (bf16[8,48,1024]{2,1,0:T(8,128)(2,1)S(1)}, bf16[8,48,1024]{2,1,0:T(8,128)(2,1)S(1)}, u32[]{:S(2)}, u32[]{:S(2)}) collective-permute-start(bf16[8,48,1024]{2,1,0:T(8,128)(2,1)S(1)} %pad_maximum_fusion.1.refs_9_.refs_6_), channel_id=1, source_target_pairs={{0,1},{1,0},{2,3},{3,2},{4,5},{5,4},{6,7},{7,6},{8,9},{9,8},{10,11... | collective-permute-start | bytes 2359304 | tf_op jit(solution)/shard_map/ppermute | solution.py:478
  47.7 12.0 %collective-permute-start.9 = (bf16[8,48,1024]{2,1,0:T(8,128)(2,1)S(1)}, bf16[8,48,1024]{2,1,0:T(8,128)(2,1)S(1)}, u32[]{:S(2)}, u32[]{:S(2)}) collective-permute-start(bf16[8,48,1024]{2,1,0:T(8,128)(2,1)S(1)} %pad_maximum_fusion.2.refs_11_.refs_8_), channel_id=1, source_target_pairs={{0,2},{1,3},{2,0},{3,1},{4,6},{5,7},{6,4},{7,5},{8,10},{9,11},{10,... | collective-permute-start | bytes 2359304 | tf_op jit(solution)/shard_map/ppermute | solution.py:478
  60.4 4.4 %collective-permute-start.10 = (bf16[512,768]{1,0:T(8,128)(2,1)}, bf16[512,768]{1,0:T(8,128)(2,1)S(1)}, u32[]{:S(2)}, u32[]{:S(2)}) collective-permute-start(bf16[512,768]{1,0:T(8,128)(2,1)} %get-tuple-element.66.refs_10_), channel_id=1, source_target_pairs={{16,0},{17,1},{18,2},{19,3},{20,4},{21,5},{22,6},{23,7},{24,8},{25... | collective-permute-start | bytes 2359304 | tf_op jit(solution)/shard_map/ppermute | solution.py:567
  76.8 16.3 %collective-permute-start.11 = (bf16[8,48,1024]{2,1,0:T(8,128)(2,1)S(1)}, bf16[8,48,1024]{2,1,0:T(8,128)(2,1)S(1)}, u32[]{:S(2)}, u32[]{:S(2)}) collective-permute-start(bf16[8,48,1024]{2,1,0:T(8,128)(2,1)S(1)} %get-tuple-element.73), channel_id=1, source_target_pairs={{0,4},{1,5},{2,6},{3,7},{4,0},{5,1},{6,2},{7,3},{8,12},{9,13},{10,... | collective-permute-start | bytes 2359304 | tf_op jit(solution)/shard_map/ppermute | solution.py:478
  77.9 17.8 %collective-permute-start.15 = (bf16[8,48,1024]{2,1,0:T(8,128)(2,1)S(1)}, bf16[8,48,1024]{2,1,0:T(8,128)(2,1)S(1)}, u32[]{:S(2)}, u32[]{:S(2)}) collective-permute-start(bf16[8,48,1024]{2,1,0:T(8,128)(2,1)S(1)} %get-tuple-element.75), channel_id=1, source_target_pairs={{0,1},{1,0},{2,3},{3,2},{4,5},{5,4},{6,7},{7,6},{8,9},{9,8},{10,11... | collective-permute-start | bytes 2359304 | tf_op jit(solution)/shard_map/ppermute | solution.py:478
  78.2 18.6 %collective-permute-start.19 = (bf16[8,48,1024]{2,1,0:T(8,128)(2,1)S(1)}, bf16[8,48,1024]{2,1,0:T(8,128)(2,1)S(1)}, u32[]{:S(2)}, u32[]{:S(2)}) collective-permute-start(bf16[8,48,1024]{2,1,0:T(8,128)(2,1)S(1)} %get-tuple-element.77), channel_id=1, source_target_pairs={{0,2},{1,3},{2,0},{3,1},{4,6},{5,7},{6,4},{7,5},{8,10},{9,11},{10,... | collective-permute-start | bytes 2359304 | tf_op jit(solution)/shard_map/ppermute | solution.py:478
  93.2 7.8 %collective-permute-start.12 = (bf16[4,48,1024]{2,1,0:T(8,128)(2,1)S(1)}, bf16[4,48,1024]{2,1,0:T(8,128)(2,1)S(1)}, u32[]{:S(2)}, u32[]{:S(2)}) collective-permute-start(bf16[4,48,1024]{2,1,0:T(8,128)(2,1)S(1)} %add_convert_fusion.2), channel_id=1, source_target_pairs={{0,2},{1,3},{2,0},{3,1},{4,6},{5,7},{6,4},{7,5},{8,10},{9,11},{10,... | collective-permute-start | bytes 1179656 | tf_op jit(solution)/shard_map/ppermute | solution.py:478
  95.9 11.0 %collective-permute-start.16 = (bf16[4,48,1024]{2,1,0:T(8,128)(2,1)S(1)}, bf16[4,48,1024]{2,1,0:T(8,128)(2,1)S(1)}, u32[]{:S(2)}, u32[]{:S(2)}) collective-permute-start(bf16[4,48,1024]{2,1,0:T(8,128)(2,1)S(1)} %add_convert_fusion.1), channel_id=1, source_target_pairs={{0,4},{1,5},{2,6},{3,7},{4,0},{5,1},{6,2},{7,3},{8,12},{9,13},{10,... | collective-permute-start | bytes 1179656 | tf_op jit(solution)/shard_map/ppermute | solution.py:478
  96.9 11.7 %collective-permute-start.20 = (bf16[4,48,1024]{2,1,0:T(8,128)(2,1)S(1)}, bf16[4,48,1024]{2,1,0:T(8,128)(2,1)S(1)}, u32[]{:S(2)}, u32[]{:S(2)}) collective-permute-start(bf16[4,48,1024]{2,1,0:T(8,128)(2,1)S(1)} %add_convert_fusion), channel_id=1, source_target_pairs={{0,1},{1,0},{2,3},{3,2},{4,5},{5,4},{6,7},{7,6},{8,9},{9,8},{10,11... | collective-permute-start | bytes 1179656 | tf_op jit(solution)/shard_map/ppermute | solution.py:478
  101.1 8.6 %collective-permute-start.13 = (bf16[2,48,1024]{2,1,0:T(8,128)(2,1)S(1)}, bf16[2,48,1024]{2,1,0:T(8,128)(2,1)S(1)}, u32[]{:S(2)}, u32[]{:S(2)}) collective-permute-start(bf16[2,48,1024]{2,1,0:T(8,128)(2,1)S(1)} %add_convert_fusion.5), channel_id=1, source_target_pairs={{0,1},{1,0},{2,3},{3,2},{4,5},{5,4},{6,7},{7,6},{8,9},{9,8},{10,11... | collective-permute-start | bytes 589832 | tf_op jit(solution)/shard_map/ppermute | solution.py:478
  107.0 5.7 %collective-permute-start.17 = (bf16[2,48,1024]{2,1,0:T(8,128)(2,1)S(1)}, bf16[2,48,1024]{2,1,0:T(8,128)(2,1)S(1)}, u32[]{:S(2)}, u32[]{:S(2)}) collective-permute-start(bf16[2,48,1024]{2,1,0:T(8,128)(2,1)S(1)} %add_convert_fusion.4), channel_id=1, source_target_pairs={{0,2},{1,3},{2,0},{3,1},{4,6},{5,7},{6,4},{7,5},{8,10},{9,11},{10,... | collective-permute-start | bytes 589832 | tf_op jit(solution)/shard_map/ppermute | solution.py:478
  108.7 6.3 %collective-permute-start.21 = (bf16[2,48,1024]{2,1,0:T(8,128)(2,1)S(1)}, bf16[2,48,1024]{2,1,0:T(8,128)(2,1)S(1)}, u32[]{:S(2)}, u32[]{:S(2)}) collective-permute-start(bf16[2,48,1024]{2,1,0:T(8,128)(2,1)S(1)} %add_convert_fusion.3), channel_id=1, source_target_pairs={{0,4},{1,5},{2,6},{3,7},{4,0},{5,1},{6,2},{7,3},{8,12},{9,13},{10,... | collective-permute-start | bytes 589832 | tf_op jit(solution)/shard_map/ppermute | solution.py:478
  109.8 7.2 %collective-permute-start.14 = (bf16[1,48,1024]{2,1,0:T(8,128)(2,1)S(1)}, bf16[1,48,1024]{2,1,0:T(8,128)(2,1)S(1)}, u32[]{:S(2)}, u32[]{:S(2)}) collective-permute-start(bf16[1,48,1024]{2,1,0:T(8,128)(2,1)S(1)} %add_convert_fusion.8), channel_id=1, source_target_pairs={{0,8},{1,9},{2,10},{3,11},{4,12},{5,13},{6,14},{7,15},{8,0},{9,1},... | collective-permute-start | bytes 294920 | tf_op jit(solution)/shard_map/ppermute | solution.py:478
  112.8 6.6 %collective-permute-start.18 = (bf16[1,48,1024]{2,1,0:T(8,128)(2,1)S(1)}, bf16[1,48,1024]{2,1,0:T(8,128)(2,1)S(1)}, u32[]{:S(2)}, u32[]{:S(2)}) collective-permute-start(bf16[1,48,1024]{2,1,0:T(8,128)(2,1)S(1)} %add_convert_fusion.7), channel_id=1, source_target_pairs={{0,8},{1,9},{2,10},{3,11},{4,12},{5,13},{6,14},{7,15},{8,0},{9,1},... | collective-permute-start | bytes 294920 | tf_op jit(solution)/shard_map/ppermute | solution.py:478
  115.0 6.6 %collective-permute-start.22 = (bf16[1,48,1024]{2,1,0:T(8,128)(2,1)S(1)}, bf16[1,48,1024]{2,1,0:T(8,128)(2,1)S(1)}, u32[]{:S(2)}, u32[]{:S(2)}) collective-permute-start(bf16[1,48,1024]{2,1,0:T(8,128)(2,1)S(1)} %add_convert_fusion.6), channel_id=1, source_target_pairs={{0,8},{1,9},{2,10},{3,11},{4,12},{5,13},{6,14},{7,15},{8,0},{9,1},... | collective-permute-start | bytes 294920 | tf_op jit(solution)/shard_map/ppermute | solution.py:478

commit v2 on v1

--- a/solution.py
+++ b/solution.py
@@ -276,17 +276,45 @@
     return (upper_v[...].astype(F32) + inverse * (grad_standard - correction)).astype(BF16)
 
 
+def assemble_body(layout, *refs):
+    pieces, (out, sems) = zip_pieces(refs, layout)
+
+    @pl.when(jnp.logical_not(is_top()))
+    def _():
+        wait_all(start_all(weight_copies(pieces, layout, out, sems, OUT_COLUMNS)))
+
+
+def assemble(gathered, layout, width):
+    inputs = flat_pieces(gathered)
+
+    def body(*refs):
+        assemble_body(layout, *refs)
+
+    return call(
+        body,
+        shape((width, INNER)),
+        [ANY] * len(inputs),
+        ANY,
+        [pltpu.SemaphoreType.DMA((copy_count(layout, OUT_COLUMNS),))],
+        1,
+    )(*inputs)
+
+
 def section_body(layout, turn, aliased, with_input, *refs):
-    gain_ref, received, top, x, qkv, weights, context = refs[:7]
-    pieces, refs = zip_pieces(refs[7:], layout)
+    gain_ref, received, top, x, qkv, weights, context, ready_w = refs[:8]
+    pieces, refs = zip_pieces(refs[8:], layout)
     refs = refs[aliased:]
     upper_out, grad_out, input_out = refs[:3] if with_input else (*refs[:2], None)
     refs = refs[3 if with_input else 2 :]
     upper_v, out_w, gc_v, grad_v, sems, w_sems = refs[:6]
+    if not with_input and not aliased:
+        upper_v, grad_v = upper_out, grad_out
 
     @pl.when(is_turn(turn))
     def _():
-        w_copies = start_all(weight_copies(pieces, layout, out_w, w_sems, OUT_COLUMNS))
+        w_copies = []
+        if turn == 0:
+            w_copies = start_all(weight_copies(pieces, layout, out_w, w_sems, OUT_COLUMNS))
         top_copy = pltpu.make_async_copy(top, upper_v, sems.at[2])
         pl.when(is_top())(top_copy.start)
 
@@ -300,17 +328,21 @@
             late = weight_copies(pieces, layout, qkv_w, qkv_sems, QKV_COLUMNS)
             late.append(pltpu.make_async_copy(x, x_v, sems.at[3]))
         pl.when(is_top())(top_copy.wait)
-        stores = start_all([pltpu.make_async_copy(upper_v, upper_out, sems.at[0])])
+        stores = []
+        if upper_v is not upper_out:
+            stores = start_all([pltpu.make_async_copy(upper_v, upper_out, sems.at[0])])
         wait_all(w_copies)
         start_all(late)
-        gc_v[...] = dot_nn(upper_v[...], out_w[...]).astype(BF16)
+        projection = ready_w if turn else out_w
+        gc_v[...] = dot_nn(upper_v[...], projection[...]).astype(BF16)
 
         def one_pair(pair, unused):
             backward_pair(pair, qkv, weights, context, gc_v, grad_v)
             return unused
 
         lax.fori_loop(0, PAIRS, one_pair, 0, unroll=2)
-        stores += start_all([pltpu.make_async_copy(grad_v, grad_out, sems.at[1])])
+        if grad_v is not grad_out:
+            stores += start_all([pltpu.make_async_copy(grad_v, grad_out, sems.at[1])])
         if with_input:
             wait_all(late)
             out_v[...] = input_gradient(upper_v, grad_v, x_v, qkv_w, gain_ref)
@@ -318,16 +350,19 @@
         wait_all(stores)
 
 
-def section_backward(turn, with_input, gain, received, top, x, saved, gathered, layout, carry):
+def section_backward(
+    turn, with_input, gain, received, top, x, saved, ready, gathered, layout, carry
+):
     length, width = x.shape
     weights, context, qkv = saved
-    inputs = [gain, received, top, x, qkv, weights, context]
-    specs = [VMEM, VMEM, ANY, ANY, VMEM, VMEM, VMEM]
+    inputs = [gain, received, top, x, qkv, weights, context, ready]
+    specs = [VMEM, VMEM, ANY, ANY, VMEM, VMEM, VMEM, VMEM if turn else ANY]
     inputs = inputs + flat_pieces(gathered)
     outs = [shape((length, width)), shape((length, 3 * INNER))]
     outs = outs + [shape((length, width))] * with_input
     aliases = {}
-    if carry is not None:
+    direct = turn == 1 and not with_input
+    if carry is not None and not direct:
         aliases = {len(inputs) + index: index for index in range(len(outs))}
         inputs = inputs + list(carry[: len(outs)])
 
@@ -353,7 +388,7 @@
         body,
         tuple(outs),
         specs + [ANY] * (len(inputs) - len(specs)),
-        (ANY,) * len(outs),
+        (VMEM if direct else ANY,) * len(outs),
         scratch,
         24 if with_input else 16,
         aliases,
@@ -397,10 +432,10 @@
     )(*inputs)
 
 
-def term_body(layout, rows, normed, upper, grad, context, *refs):
+def fill_terms(layout, rows, operands, outs, scratch):
+    normed, upper, grad, context = operands
+    upper_t, normed_v, upper_v = scratch
     position = lax.axis_index("dp")
-    count = 2 * len(layout[1])
-    outs, (upper_t, normed_v, upper_v) = refs[:count], refs[count:]
     upper_t[...] = upper[...].T
     for chunk, (order, (start, stop)) in enumerate(zip(*layout)):
         half = len(order) // 2
@@ -411,7 +446,8 @@
                 normed_v[own] = normed[source]
             if stop > 3 * INNER:
                 upper_v[own] = upper_t[source]
-        for out, side in ((outs[2 * chunk + 1], 1), (outs[2 * chunk], 0)):
+        for side in (1, 0):
+            out = outs[2 * chunk + side]
             at = slice(side * half * rows, (side + 1) * half * rows)
 
             def store(value, low, high, out=out):
@@ -428,28 +464,50 @@
                 store(dot_nn(upper_v[at], part), low, stop)
 
 
-def weight_terms(normed, upper, grad, context, rows, layout):
+def top_term_body(layout, rows, *refs):
+    count = 2 * len(layout[1])
+
+    @pl.when(is_top())
+    def _():
+        outs, scratch = refs[4 : 4 + count], refs[4 + count :]
+        fill_terms(layout, rows, refs[:4], outs, scratch)
+
+
+def lower_term_body(layout, rows, *refs):
+    count = 2 * len(layout[1])
+    kept, outs, scratch = refs[4 : 4 + count], refs[4 + count : 4 + 2 * count], refs[4 + 2 * count :]
+
+    @pl.when(is_top())
+    def _():
+        for source, out in zip(kept, outs):
+            out[...] = source[...]
+
+    @pl.when(jnp.logical_not(is_top()))
+    def _():
+        fill_terms(layout, rows, refs[:4], outs, scratch)
+
+
+def weight_terms(normed, upper, grad, context, rows, layout, carry):
     width, length = normed.shape
-    inputs = [normed, upper, grad, context]
     orders, columns = layout
     count = len(orders[0])
-    outs = tuple(
-        shape((count // 2, rows, stop - start)) for start, stop in columns for _ in range(2)
-    )
-
-    def body(*refs):
-        term_body(layout, rows, *refs)
+    dims = [(count // 2, rows, stop - start) for start, stop in columns for _ in range(2)]
+    inputs = [normed, upper, grad, context]
+    scratch = [pltpu.VMEM((width, length), BF16)] * 3
+    body = top_term_body
+    if carry is not None:
+        inputs = inputs + list(carry)
+        body = lower_term_body
+
+    def bound(*refs):
+        body(layout, rows, *refs)
 
     return call(
-        body,
-        outs,
+        bound,
+        tuple(shape(each) for each in dims),
         [VMEM] * len(inputs),
-        (VMEM,) * len(outs),
-        [
-            pltpu.VMEM((width, length), BF16),
-            pltpu.VMEM((width, length), BF16),
-            pltpu.VMEM((width, length), BF16),
-        ],
+        (VMEM,) * len(dims),
+        scratch,
         24,
     )(*inputs)
 
@@ -458,6 +516,12 @@
     bits = [1 << b for b in range(count.bit_length() - 1)]
     near, far = bits[:free], bits[free:][::-1]
     return [far + near[c:] + near[:c] for c in range(free)]
+
+
+def scatter_orders(count, free):
+    bits = [1 << b for b in range(count.bit_length() - 1)]
+    near, far = bits[:free][::-1], bits[free:][::-1]
+    return [far + near[-c:] + near[:-c] for c in range(free)]
 
 
 def slot_offsets(order):
@@ -557,21 +621,27 @@
         gather.advance()
     pieces = (gather.final, gather.layout)
 
+    ready = assemble(*pieces, x.shape[1])
+
     received = top
-    carry = None
+    carry = terms = None
+    back = scatter_orders(replicas, 3)
+    layout = exchange_layout(total, back)
     for turn in range(sections):
         below = turn + 1 < sections
-        kept = section_backward(turn, below, ln_gain, received, top, x, saved, *pieces, carry)
+        kept = section_backward(
+            turn, below, ln_gain, received, top, x, saved, ready if turn else top, *pieces, carry
+        )
         carry = [*kept, *(carry or kept)[len(kept) :]]
         if below:
             received = lax.ppermute(
                 carry[2], "pipe", [(source, source - 1) for source in range(1, sections)]
             )
+        if turn == 0:
+            terms = weight_terms(normed, *carry[:2], saved[1], rows, layout, None)
     upper, grad, grad_input = carry
-    terms = weight_terms(
-        normed, upper, grad, saved[1], rows, exchange_layout(total, orders)
-    )
-    summed = scatter_rows(terms, orders, 1.0 / replicas)
+    terms = weight_terms(normed, upper, grad, saved[1], rows, layout, terms)
+    summed = scatter_rows(terms, back, 1.0 / replicas)
     grad_input = project(sections - 1, ln_gain, upper, x, grad, *pieces, grad_input)
     return (grad_input[None, None], summed[None])
 

time: 123 us -> 121 us (0.984)
  starting transfers between devices: 33.2 us -> 31.6 us
    ppermute x22, starting transfers between devices: 31.9 us -> 30.4 us  [across(): lax.ppermute(value, 'dp', [(source, source ^ bit) for source in range(cou...]
    pallas_call x3 -> x5, Pallas kernels: 12.7 us -> 12.6 us  [the longest x2 9.47 us: section_backward(): call(body, tuple(outs), specs + [ANY] * (len(inputs) - len(specs)), (VMEM...]
where the time goes in v2:
time: 121 us; the launch traced here: 120 us
  waiting for transfers between devices  53.8 us (44%)
  starting transfers between devices  31.6 us (26%)
  Pallas kernels  29.7 us (25%)
  other arithmetic  2.24 us (2%)
  local copies, waits for them, and re-layouts  2.19 us (2%)
    ppermute x22, waiting for transfers between devices, across(): lax.ppermute(value, 'dp', [(source, source ^ bit) for source in range(cou...  51.2 us
    ppermute x22, starting transfers between devices, across(): lax.ppermute(value, 'dp', [(source, source ^ bit) for source in range(cou...  30.4 us
    pallas_call x4, Pallas kernels, forward(): call(body, (shape((HEADS, length, length)), shape((length, INNER)), shape...  11.6 us
    pallas_call x2, Pallas kernels, section_backward(): call(body, tuple(outs), specs + [ANY] * (len(inputs) - len(specs)), (VMEM...  9.47 us
    pallas_call x1, Pallas kernels, project(): call(body, shape((length, width)), [VMEM] * 3 + [ANY] * (len(inputs) - 3)...  4.89 us
    pallas_call x2, Pallas kernels, weight_terms(): call(bound, tuple((shape(each) for each in dims)), [VMEM] * len(inputs),...  2.65 us
    ppermute x1, waiting for transfers between devices, on_device(): lax.ppermute(carry[2], 'pipe', [(source, source - 1) for source in range(...  2.58 us
  transfers between devices with their start and end apart: 23, of which 16 were waited for; matrix products, arithmetic and copies ran while one was open for 1% of the time, Pallas kernels for 5%

profile of v2, /device:TPU:0, one launch (start us, length us, event | category | flops | bytes accessed | tf_op | source)
XLA Modules:
  0.0 120.5 jit_solution(1355747093175132978)
XLA Ops:
  0.7 1.0 copy.18
  1.6 11.3 %shard_map.77 = (bf16[12,512,512]{2,1,0:T(8,128)(2,1)S(1)}, bf16[512,768]{1,0:T(8,128)(2,1)S(1)}, bf16[512,2304]{1,0:T(8,128)(2,1)S(1)}) custom-call(s32[12,6,3]{2,1,0:T(8,128)S(1)} %bitcast.17, bf16[512,2304]{1,0:T(8,128)(2,1)} %bitcast.5), custom_call_target="tpu_custom_call" | custom-call | tf_op jit(solution)/shard_map/pallas_call | solution.py:167
  13.0 4.1 %collective-permute-start = (bf16[1,48,3072]{2,1,0:T(8,128)(2,1)}, bf16[1,48,3072]{2,1,0:T(8,128)(2,1)S(1)}, u32[]{:S(2)}, u32[]{:S(2)}) collective-permute-start(bf16[1,48,3072]{2,1,0:T(8,128)(2,1)} %param.9), channel_id=1, source_target_pairs={{0,8},{1,9},{2,10},{3,11},{4,12},{5,13},{6,14},{7,15},{8,0},{9,1},... | collective-permute-start | bytes 884744 | tf_op jit(solution)/shard_map/ppermute | solution.py:542
  17.1 1.1 copy-done.2
  18.2 0.7 shard_map.79.refs_0_
  19.0 6.3 %collective-permute-done = bf16[1,48,3072]{2,1,0:T(8,128)(2,1)S(1)} collective-permute-done((bf16[1,48,3072]{2,1,0:T(8,128)(2,1)}, bf16[1,48,3072]{2,1,0:T(8,128)(2,1)S(1)}, u32[]{:S(2)}, u32[]{:S(2)}) %collective-permute-start) | collective-permute-done | bytes 294944 | tf_op jit(solution)/shard_map/ppermute | solution.py:542
  25.4 1.1 collective-permute-start.5
  26.5 1.5 %collective-permute-start.3 = (bf16[2,48,1024]{2,1,0:T(8,128)(2,1)S(1)}, bf16[2,48,1024]{2,1,0:T(8,128)(2,1)S(1)}, u32[]{:S(2)}, u32[]{:S(2)}) collective-permute-start(bf16[2,48,1024]{2,1,0:T(8,128)(2,1)S(1)} %get-tuple-element.91), channel_id=1, source_target_pairs={{0,2},{1,3},{2,0},{3,1},{4,6},{5,7},{6,4},{7,5},{8,10},{9,11},{10,... | collective-permute-start | bytes 589832 | tf_op jit(solution)/shard_map/ppermute | solution.py:542
  28.0 1.5 %collective-permute-start.1 = (bf16[2,48,1024]{2,1,0:T(8,128)(2,1)S(1)}, bf16[2,48,1024]{2,1,0:T(8,128)(2,1)S(1)}, u32[]{:S(2)}, u32[]{:S(2)}) collective-permute-start(bf16[2,48,1024]{2,1,0:T(8,128)(2,1)S(1)} %get-tuple-element.92), channel_id=1, source_target_pairs={{0,1},{1,0},{2,3},{3,2},{4,5},{5,4},{6,7},{7,6},{8,9},{9,8},{10,11... | collective-permute-start | bytes 589832 | tf_op jit(solution)/shard_map/ppermute | solution.py:542
  29.5 2.4 %collective-permute-done.5 = bf16[2,48,1024]{2,1,0:T(8,128)(2,1)S(1)} collective-permute-done((bf16[2,48,1024]{2,1,0:T(8,128)(2,1)S(1)}, bf16[2,48,1024]{2,1,0:T(8,128)(2,1)S(1)}, u32[]{:S(2)}, u32[]{:S(2)}) %collective-permute-start.5) | collective-permute-done | bytes 196640 | tf_op jit(solution)/shard_map/ppermute | solution.py:542
  31.9 2.5 %collective-permute-start.6 = (bf16[4,48,1024]{2,1,0:T(8,128)(2,1)S(1)}, bf16[4,48,1024]{2,1,0:T(8,128)(2,1)S(1)}, u32[]{:S(2)}, u32[]{:S(2)}) collective-permute-start(bf16[4,48,1024]{2,1,0:T(8,128)(2,1)S(1)} %pad_maximum_fusion.6), channel_id=1, source_target_pairs={{0,1},{1,0},{2,3},{3,2},{4,5},{5,4},{6,7},{7,6},{8,9},{9,8},{10,11... | collective-permute-start | bytes 1179656 | tf_op jit(solution)/shard_map/ppermute | solution.py:542
  34.4 0.7 collective-permute-start.4
  35.1 0.6 collective-permute-done.1
  35.8 0.9 collective-permute-start.2
  36.8 7.6 %collective-permute-done.6 = bf16[4,48,1024]{2,1,0:T(8,128)(2,1)S(1)} collective-permute-done((bf16[4,48,1024]{2,1,0:T(8,128)(2,1)S(1)}, bf16[4,48,1024]{2,1,0:T(8,128)(2,1)S(1)}, u32[]{:S(2)}, u32[]{:S(2)}) %collective-permute-start.6) | collective-permute-done | bytes 393248 | tf_op jit(solution)/shard_map/ppermute | solution.py:542
  44.9 1.1 collective-permute-start.7
  45.9 1.8 %collective-permute-start.8 = (bf16[8,48,1024]{2,1,0:T(8,128)(2,1)S(1)}, bf16[8,48,1024]{2,1,0:T(8,128)(2,1)S(1)}, u32[]{:S(2)}, u32[]{:S(2)}) collective-permute-start(bf16[8,48,1024]{2,1,0:T(8,128)(2,1)S(1)} %pad_maximum_fusion.1.refs_10_.refs_2_.refs_6_), channel_id=1, source_target_pairs={{0,1},{1,0},{2,3},{3,2},{4,5},{5,4},{6,7},{7,6},{8,9},{9,8},{10,11... | collective-permute-start | bytes 2359304 | tf_op jit(solution)/shard_map/ppermute | solution.py:542
  47.7 1.5 %collective-permute-start.9 = (bf16[8,48,1024]{2,1,0:T(8,128)(2,1)S(1)}, bf16[8,48,1024]{2,1,0:T(8,128)(2,1)S(1)}, u32[]{:S(2)}, u32[]{:S(2)}) collective-permute-start(bf16[8,48,1024]{2,1,0:T(8,128)(2,1)S(1)} %pad_maximum_fusion.2.refs_12_.refs_4_.refs_8_), channel_id=1, source_target_pairs={{0,2},{1,3},{2,0},{3,1},{4,6},{5,7},{6,4},{7,5},{8,10},{9,11},{10,... | collective-permute-start | bytes 2359304 | tf_op jit(solution)/shard_map/ppermute | solution.py:542
  49.4 7.6 %collective-permute-done.7.refs_9_.refs_1_.refs_5_ = bf16[8,48,1024]{2,1,0:T(8,128)(2,1)S(1)} collective-permute-done((bf16[8,48,1024]{2,1,0:T(8,128)(2,1)S(1)}, bf16[8,48,1024]{2,1,0:T(8,128)(2,1)S(1)}, u32[]{:S(2)}, u32[]{:S(2)}) %collective-permute-start.7) | collective-permute-done | bytes 786464 | tf_op jit(solution)/shard_map/ppermute | solution.py:542
  56.9 1.0 collective-permute-done.8.refs_11_.refs_3_.refs_7_
  57.9 1.8 %collective-permute-done.9.refs_13_.refs_5_.refs_9_ = bf16[8,48,1024]{2,1,0:T(8,128)(2,1)S(1)} collective-permute-done((bf16[8,48,1024]{2,1,0:T(8,128)(2,1)S(1)}, bf16[8,48,1024]{2,1,0:T(8,128)(2,1)S(1)}, u32[]{:S(2)}, u32[]{:S(2)}) %collective-permute-start.9) | collective-permute-done | bytes 786464 | tf_op jit(solution)/shard_map/ppermute | solution.py:542
  59.7 0.6 shard_map.82
  60.4 1.3 %collective-permute-start.10 = (bf16[512,768]{1,0:T(8,128)(2,1)}, bf16[512,768]{1,0:T(8,128)(2,1)S(1)}, u32[]{:S(2)}, u32[]{:S(2)}) collective-permute-start(bf16[512,768]{1,0:T(8,128)(2,1)} %get-tuple-element.72.refs_10_), channel_id=1, source_target_pairs={{16,0},{17,1},{18,2},{19,3},{20,4},{21,5},{22,6},{23,7},{24,8},{25... | collective-permute-start | bytes 2359304 | tf_op jit(solution)/shard_map/ppermute | solution.py:637
  61.7 0.5 shard_map.83.refs_7_
  62.2 2.6 %collective-permute-done.10.refs_1_ = bf16[512,768]{1,0:T(8,128)(2,1)S(1)} collective-permute-done((bf16[512,768]{1,0:T(8,128)(2,1)}, bf16[512,768]{1,0:T(8,128)(2,1)S(1)}, u32[]{:S(2)}, u32[]{:S(2)}) %collective-permute-start.10) | collective-permute-done | bytes 786464 | tf_op jit(solution)/shard_map/ppermute | solution.py:637
  64.8 8.9 %shard_map.84 = (bf16[512,768]{1,0:T(8,128)(2,1)S(1)}, bf16[512,2304]{1,0:T(8,128)(2,1)S(1)}) custom-call(f32[1,768]{1,0:T(1,128)S(1)} %copy-done.4, bf16[512,768]{1,0:T(8,128)(2,1)S(1)} %collective-permute-done.10.refs_1_, bf16[512,768]{1,0:T(8,128)(2,1)S(1)} %bitcast.12, bf16[512,768]{1,0:T(8,128)(2,1)S(1)} %bitcast.15, ...), custom_call_target="tpu_custom_call" | custom-call | tf_op jit(solution)/shard_map/pallas_call | solution.py:387
  73.6 2.6 %shard_map.87 = (bf16[8,48,1024]{2,1,0:T(8,128)(2,1)S(1)}, bf16[8,48,1024]{2,1,0:T(8,128)(2,1)S(1)}, bf16[8,48,1024]{2,1,0:T(8,128)(2,1)S(1)}, bf16[8,48,1024]{2...) custom-call(bf16[768,512]{1,0:T(8,128)(2,1)S(1)} %shard_map.79.refs_0_, ...), custom_call_target="tpu_custom_call" | custom-call | tf_op jit(solution)/shard_map/pallas_call | solution.py:505
  76.3 0.3 collective-permute-start.11
  76.6 1.8 %collective-permute-start.15 = (bf16[8,48,1024]{2,1,0:T(8,128)(2,1)S(1)}, bf16[8,48,1024]{2,1,0:T(8,128)(2,1)S(1)}, u32[]{:S(2)}, u32[]{:S(2)}) collective-permute-start(bf16[8,48,1024]{2,1,0:T(8,128)(2,1)S(1)} %get-tuple-element.87), channel_id=1, source_target_pairs={{0,2},{1,3},{2,0},{3,1},{4,6},{5,7},{6,4},{7,5},{8,10},{9,11},{10,... | collective-permute-start | bytes 2359304 | tf_op jit(solution)/shard_map/ppermute | solution.py:542
  78.4 0.8 collective-permute-start.19
  79.2 4.9 %shard_map.85 = bf16[512,768]{1,0:T(8,128)(2,1)} custom-call(f32[1,768]{1,0:T(1,128)S(1)} %copy-done.4, bf16[512,768]{1,0:T(8,128)(2,1)S(1)} %get-tuple-element.73.refs_1_, bf16[512,2304]{1,0:T(8,128)(2,1)S(1)} %get-tuple-element.74.refs_2_, bf16[512,768]{1,0:T(8,128)(2,1)S(1)} %bitcast.16, ...), custom_call_target="tpu_custom_call", output_to_operand_aliasing={{}: (10, {})} | custom-call | tf_op jit(solution)/shard_map/pallas_call | solution.py:418
  84.1 8.9 %collective-permute-done.11 = bf16[8,48,1024]{2,1,0:T(8,128)(2,1)S(1)} collective-permute-done((bf16[8,48,1024]{2,1,0:T(8,128)(2,1)S(1)}, bf16[8,48,1024]{2,1,0:T(8,128)(2,1)S(1)}, u32[]{:S(2)}, u32[]{:S(2)}) %collective-permute-start.11) | collective-permute-done | bytes 786464 | tf_op jit(solution)/shard_map/ppermute | solution.py:542
  93.1 1.8 %collective-permute-start.12 = (bf16[4,48,1024]{2,1,0:T(8,128)(2,1)S(1)}, bf16[4,48,1024]{2,1,0:T(8,128)(2,1)S(1)}, u32[]{:S(2)}, u32[]{:S(2)}) collective-permute-start(bf16[4,48,1024]{2,1,0:T(8,128)(2,1)S(1)} %add_convert_fusion.2), channel_id=1, source_target_pairs={{0,2},{1,3},{2,0},{3,1},{4,6},{5,7},{6,4},{7,5},{8,10},{9,11},{10,... | collective-permute-start | bytes 1179656 | tf_op jit(solution)/shard_map/ppermute | solution.py:542
  95.0 1.5 %collective-permute-start.16 = (bf16[4,48,1024]{2,1,0:T(8,128)(2,1)S(1)}, bf16[4,48,1024]{2,1,0:T(8,128)(2,1)S(1)}, u32[]{:S(2)}, u32[]{:S(2)}) collective-permute-start(bf16[4,48,1024]{2,1,0:T(8,128)(2,1)S(1)} %add_convert_fusion.1), channel_id=1, source_target_pairs={{0,4},{1,5},{2,6},{3,7},{4,0},{5,1},{6,2},{7,3},{8,12},{9,13},{10,... | collective-permute-start | bytes 1179656 | tf_op jit(solution)/shard_map/ppermute | solution.py:542
  96.6 0.3 collective-permute-start.20
  96.8 4.1 %collective-permute-done.12 = bf16[4,48,1024]{2,1,0:T(8,128)(2,1)S(1)} collective-permute-done((bf16[4,48,1024]{2,1,0:T(8,128)(2,1)S(1)}, bf16[4,48,1024]{2,1,0:T(8,128)(2,1)S(1)}, u32[]{:S(2)}, u32[]{:S(2)}) %collective-permute-start.12) | collective-permute-done | bytes 393248 | tf_op jit(solution)/shard_map/ppermute | solution.py:542
  101.0 1.2 collective-permute-start.13
  102.1 3.8 %collective-permute-done.16 = bf16[4,48,1024]{2,1,0:T(8,128)(2,1)S(1)} collective-permute-done((bf16[4,48,1024]{2,1,0:T(8,128)(2,1)S(1)}, bf16[4,48,1024]{2,1,0:T(8,128)(2,1)S(1)}, u32[]{:S(2)}, u32[]{:S(2)}) %collective-permute-start.16) | collective-permute-done | bytes 393248 | tf_op jit(solution)/shard_map/ppermute | solution.py:542
  106.0 0.6 collective-permute-start.17
  106.7 0.4 collective-permute-start.21
  107.1 1.0 collective-permute-done.13
  108.1 2.1 %collective-permute-start.14 = (bf16[1,48,1024]{2,1,0:T(8,128)(2,1)S(1)}, bf16[1,48,1024]{2,1,0:T(8,128)(2,1)S(1)}, u32[]{:S(2)}, u32[]{:S(2)}) collective-permute-start(bf16[1,48,1024]{2,1,0:T(8,128)(2,1)S(1)} %add_convert_fusion.8), channel_id=1, source_target_pairs={{0,8},{1,9},{2,10},{3,11},{4,12},{5,13},{6,14},{7,15},{8,0},{9,1},... | collective-permute-start | bytes 294920 | tf_op jit(solution)/shard_map/ppermute | solution.py:542
  110.2 1.6 %collective-permute-done.17 = bf16[2,48,1024]{2,1,0:T(8,128)(2,1)S(1)} collective-permute-done((bf16[2,48,1024]{2,1,0:T(8,128)(2,1)S(1)}, bf16[2,48,1024]{2,1,0:T(8,128)(2,1)S(1)}, u32[]{:S(2)}, u32[]{:S(2)}) %collective-permute-start.17) | collective-permute-done | bytes 196640 | tf_op jit(solution)/shard_map/ppermute | solution.py:542
  111.8 2.1 %collective-permute-start.18 = (bf16[1,48,1024]{2,1,0:T(8,128)(2,1)S(1)}, bf16[1,48,1024]{2,1,0:T(8,128)(2,1)S(1)}, u32[]{:S(2)}, u32[]{:S(2)}) collective-permute-start(bf16[1,48,1024]{2,1,0:T(8,128)(2,1)S(1)} %add_convert_fusion.7), channel_id=1, source_target_pairs={{0,8},{1,9},{2,10},{3,11},{4,12},{5,13},{6,14},{7,15},{8,0},{9,1},... | collective-permute-start | bytes 294920 | tf_op jit(solution)/shard_map/ppermute | solution.py:542
  114.0 1.0 collective-permute-start.22
  115.0 2.4 %collective-permute-done.18 = bf16[1,48,1024]{2,1,0:T(8,128)(2,1)S(1)} collective-permute-done((bf16[1,48,1024]{2,1,0:T(8,128)(2,1)S(1)}, bf16[1,48,1024]{2,1,0:T(8,128)(2,1)S(1)}, u32[]{:S(2)}, u32[]{:S(2)}) %collective-permute-start.18) | collective-permute-done | bytes 98336 | tf_op jit(solution)/shard_map/ppermute | solution.py:542
  117.5 2.1 %collective-permute-done.22 = bf16[1,48,1024]{2,1,0:T(8,128)(2,1)S(1)} collective-permute-done((bf16[1,48,1024]{2,1,0:T(8,128)(2,1)S(1)}, bf16[1,48,1024]{2,1,0:T(8,128)(2,1)S(1)}, u32[]{:S(2)}, u32[]{:S(2)}) %collective-permute-start.22) | collective-permute-done | bytes 98336 | tf_op jit(solution)/shard_map/ppermute | solution.py:542
  119.6 0.9 maximum_multiply_fusion
  (43 shorter events, 1.9 us)
Async XLA Ops:
  0.6 18.2 %copy-start = (bf16[1,1,512,2304]{3,2,1,0:T(8,128)(2,1)S(1)}, bf16[1,1,512,2304]{3,2,1,0:T(8,128)(2,1)}, u32[]{:S(2)}) copy-start(bf16[1,1,512,2304]{3,2,1,0:T(8,128)(2,1)} %param.7) | copy-start | bytes 7077892
  0.6 16.4 %copy-start.4 = (f32[1,768]{1,0:T(1,128)S(1)}, f32[1,768]{1,0:T(1,128)}, u32[]{:S(2)}) copy-start(f32[1,768]{1,0:T(1,128)} %refs_0_.5) | copy-start | bytes 9220
  13.0 12.3 %collective-permute-start = (bf16[1,48,3072]{2,1,0:T(8,128)(2,1)}, bf16[1,48,3072]{2,1,0:T(8,128)(2,1)S(1)}, u32[]{:S(2)}, u32[]{:S(2)}) collective-permute-start(bf16[1,48,3072]{2,1,0:T(8,128)(2,1)} %param.9), channel_id=1, source_target_pairs={{0,8},{1,9},{2,10},{3,11},{4,12},{5,13},{6,14},{7,15},{8,0},{9,1},... | collective-permute-start | bytes 884744 | tf_op jit(solution)/shard_map/ppermute | solution.py:542
  17.1 1.1 copy-start.2
  18.9 6.4 %copy-start.5 = (bf16[1,48,3072]{2,1,0:T(8,128)(2,1)S(1)}, bf16[1,48,3072]{2,1,0:T(8,128)(2,1)}, u32[]{:S(2)}) copy-start(bf16[1,48,3072]{2,1,0:T(8,128)(2,1)} %param.9) | copy-start | bytes 884740
  25.4 6.5 %collective-permute-start.5 = (bf16[2,48,1024]{2,1,0:T(8,128)(2,1)S(1)}, bf16[2,48,1024]{2,1,0:T(8,128)(2,1)S(1)}, u32[]{:S(2)}, u32[]{:S(2)}) collective-permute-start(bf16[2,48,1024]{2,1,0:T(8,128)(2,1)S(1)} %get-tuple-element.90), channel_id=1, source_target_pairs={{0,4},{1,5},{2,6},{3,7},{4,0},{5,1},{6,2},{7,3},{8,12},{9,13},{10,... | collective-permute-start | bytes 589832 | tf_op jit(solution)/shard_map/ppermute | solution.py:542
  26.5 7.9 %collective-permute-start.3 = (bf16[2,48,1024]{2,1,0:T(8,128)(2,1)S(1)}, bf16[2,48,1024]{2,1,0:T(8,128)(2,1)S(1)}, u32[]{:S(2)}, u32[]{:S(2)}) collective-permute-start(bf16[2,48,1024]{2,1,0:T(8,128)(2,1)S(1)} %get-tuple-element.91), channel_id=1, source_target_pairs={{0,2},{1,3},{2,0},{3,1},{4,6},{5,7},{6,4},{7,5},{8,10},{9,11},{10,... | collective-permute-start | bytes 589832 | tf_op jit(solution)/shard_map/ppermute | solution.py:542
  28.0 7.8 %collective-permute-start.1 = (bf16[2,48,1024]{2,1,0:T(8,128)(2,1)S(1)}, bf16[2,48,1024]{2,1,0:T(8,128)(2,1)S(1)}, u32[]{:S(2)}, u32[]{:S(2)}) collective-permute-start(bf16[2,48,1024]{2,1,0:T(8,128)(2,1)S(1)} %get-tuple-element.92), channel_id=1, source_target_pairs={{0,1},{1,0},{2,3},{3,2},{4,5},{5,4},{6,7},{7,6},{8,9},{9,8},{10,11... | collective-permute-start | bytes 589832 | tf_op jit(solution)/shard_map/ppermute | solution.py:542
  31.9 12.5 %collective-permute-start.6 = (bf16[4,48,1024]{2,1,0:T(8,128)(2,1)S(1)}, bf16[4,48,1024]{2,1,0:T(8,128)(2,1)S(1)}, u32[]{:S(2)}, u32[]{:S(2)}) collective-permute-start(bf16[4,48,1024]{2,1,0:T(8,128)(2,1)S(1)} %pad_maximum_fusion.6), channel_id=1, source_target_pairs={{0,1},{1,0},{2,3},{3,2},{4,5},{5,4},{6,7},{7,6},{8,9},{9,8},{10,11... | collective-permute-start | bytes 1179656 | tf_op jit(solution)/shard_map/ppermute | solution.py:542
  34.4 10.1 %collective-permute-start.4 = (bf16[4,48,1024]{2,1,0:T(8,128)(2,1)S(1)}, bf16[4,48,1024]{2,1,0:T(8,128)(2,1)S(1)}, u32[]{:S(2)}, u32[]{:S(2)}) collective-permute-start(bf16[4,48,1024]{2,1,0:T(8,128)(2,1)S(1)} %pad_maximum_fusion.5), channel_id=1, source_target_pairs={{0,4},{1,5},{2,6},{3,7},{4,0},{5,1},{6,2},{7,3},{8,12},{9,13},{10,... | collective-permute-start | bytes 1179656 | tf_op jit(solution)/shard_map/ppermute | solution.py:542
  35.8 9.0 %collective-permute-start.2 = (bf16[4,48,1024]{2,1,0:T(8,128)(2,1)S(1)}, bf16[4,48,1024]{2,1,0:T(8,128)(2,1)S(1)}, u32[]{:S(2)}, u32[]{:S(2)}) collective-permute-start(bf16[4,48,1024]{2,1,0:T(8,128)(2,1)S(1)} %pad_maximum_fusion.4), channel_id=1, source_target_pairs={{0,2},{1,3},{2,0},{3,1},{4,6},{5,7},{6,4},{7,5},{8,10},{9,11},{10,... | collective-permute-start | bytes 1179656 | tf_op jit(solution)/shard_map/ppermute | solution.py:542
  44.9 14.9 %copy-start.1 = (bf16[1,512,768]{2,1,0:T(8,128)(2,1)S(1)}, bf16[1,512,768]{2,1,0:T(8,128)(2,1)}, u32[]{:S(2)}) copy-start(bf16[1,512,768]{2,1,0:T(8,128)(2,1)} %param.11) | copy-start | bytes 2359300
  44.9 14.9 %copy-start.3 = (bf16[1,1,512,768]{3,2,1,0:T(8,128)(2,1)S(1)}, bf16[1,1,512,768]{3,2,1,0:T(8,128)(2,1)}, u32[]{:S(2)}) copy-start(bf16[1,1,512,768]{3,2,1,0:T(8,128)(2,1)} %param.6) | copy-start | bytes 2359300
  44.9 12.1 %collective-permute-start.7 = (bf16[8,48,1024]{2,1,0:T(8,128)(2,1)S(1)}, bf16[8,48,1024]{2,1,0:T(8,128)(2,1)S(1)}, u32[]{:S(2)}, u32[]{:S(2)}) collective-permute-start(bf16[8,48,1024]{2,1,0:T(8,128)(2,1)S(1)} %pad_maximum_fusion.refs_8_.refs_0_.refs_4_), channel_id=1, source_target_pairs={{0,4},{1,5},{2,6},{3,7},{4,0},{5,1},{6,2},{7,3},{8,12},{9,13},{10,... | collective-permute-start | bytes 2359304 | tf_op jit(solution)/shard_map/ppermute | solution.py:542
  45.9 12.0 %collective-permute-start.8 = (bf16[8,48,1024]{2,1,0:T(8,128)(2,1)S(1)}, bf16[8,48,1024]{2,1,0:T(8,128)(2,1)S(1)}, u32[]{:S(2)}, u32[]{:S(2)}) collective-permute-start(bf16[8,48,1024]{2,1,0:T(8,128)(2,1)S(1)} %pad_maximum_fusion.1.refs_10_.refs_2_.refs_6_), channel_id=1, source_target_pairs={{0,1},{1,0},{2,3},{3,2},{4,5},{5,4},{6,7},{7,6},{8,9},{9,8},{10,11... | collective-permute-start | bytes 2359304 | tf_op jit(solution)/shard_map/ppermute | solution.py:542
  47.7 12.0 %collective-permute-start.9 = (bf16[8,48,1024]{2,1,0:T(8,128)(2,1)S(1)}, bf16[8,48,1024]{2,1,0:T(8,128)(2,1)S(1)}, u32[]{:S(2)}, u32[]{:S(2)}) collective-permute-start(bf16[8,48,1024]{2,1,0:T(8,128)(2,1)S(1)} %pad_maximum_fusion.2.refs_12_.refs_4_.refs_8_), channel_id=1, source_target_pairs={{0,2},{1,3},{2,0},{3,1},{4,6},{5,7},{6,4},{7,5},{8,10},{9,11},{10,... | collective-permute-start | bytes 2359304 | tf_op jit(solution)/shard_map/ppermute | solution.py:542
  60.4 4.4 %collective-permute-start.10 = (bf16[512,768]{1,0:T(8,128)(2,1)}, bf16[512,768]{1,0:T(8,128)(2,1)S(1)}, u32[]{:S(2)}, u32[]{:S(2)}) collective-permute-start(bf16[512,768]{1,0:T(8,128)(2,1)} %get-tuple-element.72.refs_10_), channel_id=1, source_target_pairs={{16,0},{17,1},{18,2},{19,3},{20,4},{21,5},{22,6},{23,7},{24,8},{25... | collective-permute-start | bytes 2359304 | tf_op jit(solution)/shard_map/ppermute | solution.py:637
  76.3 16.7 %collective-permute-start.11 = (bf16[8,48,1024]{2,1,0:T(8,128)(2,1)S(1)}, bf16[8,48,1024]{2,1,0:T(8,128)(2,1)S(1)}, u32[]{:S(2)}, u32[]{:S(2)}) collective-permute-start(bf16[8,48,1024]{2,1,0:T(8,128)(2,1)S(1)} %get-tuple-element.85), channel_id=1, source_target_pairs={{0,1},{1,0},{2,3},{3,2},{4,5},{5,4},{6,7},{7,6},{8,9},{9,8},{10,11... | collective-permute-start | bytes 2359304 | tf_op jit(solution)/shard_map/ppermute | solution.py:542
  76.6 18.3 %collective-permute-start.15 = (bf16[8,48,1024]{2,1,0:T(8,128)(2,1)S(1)}, bf16[8,48,1024]{2,1,0:T(8,128)(2,1)S(1)}, u32[]{:S(2)}, u32[]{:S(2)}) collective-permute-start(bf16[8,48,1024]{2,1,0:T(8,128)(2,1)S(1)} %get-tuple-element.87), channel_id=1, source_target_pairs={{0,2},{1,3},{2,0},{3,1},{4,6},{5,7},{6,4},{7,5},{8,10},{9,11},{10,... | collective-permute-start | bytes 2359304 | tf_op jit(solution)/shard_map/ppermute | solution.py:542
  78.4 18.0 %collective-permute-start.19 = (bf16[8,48,1024]{2,1,0:T(8,128)(2,1)S(1)}, bf16[8,48,1024]{2,1,0:T(8,128)(2,1)S(1)}, u32[]{:S(2)}, u32[]{:S(2)}) collective-permute-start(bf16[8,48,1024]{2,1,0:T(8,128)(2,1)S(1)} %get-tuple-element.89), channel_id=1, source_target_pairs={{0,4},{1,5},{2,6},{3,7},{4,0},{5,1},{6,2},{7,3},{8,12},{9,13},{10,... | collective-permute-start | bytes 2359304 | tf_op jit(solution)/shard_map/ppermute | solution.py:542
  93.1 7.8 %collective-permute-start.12 = (bf16[4,48,1024]{2,1,0:T(8,128)(2,1)S(1)}, bf16[4,48,1024]{2,1,0:T(8,128)(2,1)S(1)}, u32[]{:S(2)}, u32[]{:S(2)}) collective-permute-start(bf16[4,48,1024]{2,1,0:T(8,128)(2,1)S(1)} %add_convert_fusion.2), channel_id=1, source_target_pairs={{0,2},{1,3},{2,0},{3,1},{4,6},{5,7},{6,4},{7,5},{8,10},{9,11},{10,... | collective-permute-start | bytes 1179656 | tf_op jit(solution)/shard_map/ppermute | solution.py:542
  95.0 11.0 %collective-permute-start.16 = (bf16[4,48,1024]{2,1,0:T(8,128)(2,1)S(1)}, bf16[4,48,1024]{2,1,0:T(8,128)(2,1)S(1)}, u32[]{:S(2)}, u32[]{:S(2)}) collective-permute-start(bf16[4,48,1024]{2,1,0:T(8,128)(2,1)S(1)} %add_convert_fusion.1), channel_id=1, source_target_pairs={{0,4},{1,5},{2,6},{3,7},{4,0},{5,1},{6,2},{7,3},{8,12},{9,13},{10,... | collective-permute-start | bytes 1179656 | tf_op jit(solution)/shard_map/ppermute | solution.py:542
  96.6 10.1 %collective-permute-start.20 = (bf16[4,48,1024]{2,1,0:T(8,128)(2,1)S(1)}, bf16[4,48,1024]{2,1,0:T(8,128)(2,1)S(1)}, u32[]{:S(2)}, u32[]{:S(2)}) collective-permute-start(bf16[4,48,1024]{2,1,0:T(8,128)(2,1)S(1)} %add_convert_fusion), channel_id=1, source_target_pairs={{0,1},{1,0},{2,3},{3,2},{4,5},{5,4},{6,7},{7,6},{8,9},{9,8},{10,11... | collective-permute-start | bytes 1179656 | tf_op jit(solution)/shard_map/ppermute | solution.py:542
  101.0 7.1 %collective-permute-start.13 = (bf16[2,48,1024]{2,1,0:T(8,128)(2,1)S(1)}, bf16[2,48,1024]{2,1,0:T(8,128)(2,1)S(1)}, u32[]{:S(2)}, u32[]{:S(2)}) collective-permute-start(bf16[2,48,1024]{2,1,0:T(8,128)(2,1)S(1)} %add_convert_fusion.5), channel_id=1, source_target_pairs={{0,4},{1,5},{2,6},{3,7},{4,0},{5,1},{6,2},{7,3},{8,12},{9,13},{10,... | collective-permute-start | bytes 589832 | tf_op jit(solution)/shard_map/ppermute | solution.py:542
  106.0 5.7 %collective-permute-start.17 = (bf16[2,48,1024]{2,1,0:T(8,128)(2,1)S(1)}, bf16[2,48,1024]{2,1,0:T(8,128)(2,1)S(1)}, u32[]{:S(2)}, u32[]{:S(2)}) collective-permute-start(bf16[2,48,1024]{2,1,0:T(8,128)(2,1)S(1)} %add_convert_fusion.4), channel_id=1, source_target_pairs={{0,1},{1,0},{2,3},{3,2},{4,5},{5,4},{6,7},{7,6},{8,9},{9,8},{10,11... | collective-permute-start | bytes 589832 | tf_op jit(solution)/shard_map/ppermute | solution.py:542
  106.7 7.2 %collective-permute-start.21 = (bf16[2,48,1024]{2,1,0:T(8,128)(2,1)S(1)}, bf16[2,48,1024]{2,1,0:T(8,128)(2,1)S(1)}, u32[]{:S(2)}, u32[]{:S(2)}) collective-permute-start(bf16[2,48,1024]{2,1,0:T(8,128)(2,1)S(1)} %add_convert_fusion.3), channel_id=1, source_target_pairs={{0,2},{1,3},{2,0},{3,1},{4,6},{5,7},{6,4},{7,5},{8,10},{9,11},{10,... | collective-permute-start | bytes 589832 | tf_op jit(solution)/shard_map/ppermute | solution.py:542
  108.1 6.8 %collective-permute-start.14 = (bf16[1,48,1024]{2,1,0:T(8,128)(2,1)S(1)}, bf16[1,48,1024]{2,1,0:T(8,128)(2,1)S(1)}, u32[]{:S(2)}, u32[]{:S(2)}) collective-permute-start(bf16[1,48,1024]{2,1,0:T(8,128)(2,1)S(1)} %add_convert_fusion.8), channel_id=1, source_target_pairs={{0,8},{1,9},{2,10},{3,11},{4,12},{5,13},{6,14},{7,15},{8,0},{9,1},... | collective-permute-start | bytes 294920 | tf_op jit(solution)/shard_map/ppermute | solution.py:542
  111.8 5.6 %collective-permute-start.18 = (bf16[1,48,1024]{2,1,0:T(8,128)(2,1)S(1)}, bf16[1,48,1024]{2,1,0:T(8,128)(2,1)S(1)}, u32[]{:S(2)}, u32[]{:S(2)}) collective-permute-start(bf16[1,48,1024]{2,1,0:T(8,128)(2,1)S(1)} %add_convert_fusion.7), channel_id=1, source_target_pairs={{0,8},{1,9},{2,10},{3,11},{4,12},{5,13},{6,14},{7,15},{8,0},{9,1},... | collective-permute-start | bytes 294920 | tf_op jit(solution)/shard_map/ppermute | solution.py:542
  114.0 5.6 %collective-permute-start.22 = (bf16[1,48,1024]{2,1,0:T(8,128)(2,1)S(1)}, bf16[1,48,1024]{2,1,0:T(8,128)(2,1)S(1)}, u32[]{:S(2)}, u32[]{:S(2)}) collective-permute-start(bf16[1,48,1024]{2,1,0:T(8,128)(2,1)S(1)} %add_convert_fusion.6), channel_id=1, source_target_pairs={{0,8},{1,9},{2,10},{3,11},{4,12},{5,13},{6,14},{7,15},{8,0},{9,1},... | collective-permute-start | bytes 294920 | tf_op jit(solution)/shard_map/ppermute | solution.py:542

commit v3 on v2

--- a/solution.py
+++ b/solution.py
@@ -267,9 +267,8 @@
     grad_v[:, columns_of(pair, 2, INNER)] = value_grad.astype(BF16)
 
 
-def input_gradient(upper_v, grad_v, x_v, w_v, gain_ref):
+def input_gradient(upper_v, grad_v, standard, inverse, w_v, gain_ref):
     grad_standard = dot_nt(grad_v[...], w_v[...]) * gain_ref[...]
-    standard, inverse = statistics(x_v[...])
     correction = jnp.mean(grad_standard, axis=-1, keepdims=True) + standard * jnp.mean(
         grad_standard * standard, axis=-1, keepdims=True
     )
@@ -324,13 +323,17 @@
 
         late = []
         if with_input:
-            x_v, qkv_w, out_v, qkv_sems = refs[6:]
+            x_v, qkv_w, out_v, qkv_sems, standard_v, inverse_v = refs[6:]
+            x_copy = pltpu.make_async_copy(x, x_v, sems.at[3])
+            x_copy.start()
             late = weight_copies(pieces, layout, qkv_w, qkv_sems, QKV_COLUMNS)
-            late.append(pltpu.make_async_copy(x, x_v, sems.at[3]))
         pl.when(is_top())(top_copy.wait)
         stores = []
         if upper_v is not upper_out:
             stores = start_all([pltpu.make_async_copy(upper_v, upper_out, sems.at[0])])
+        if with_input:
+            x_copy.wait()
+            standard_v[...], inverse_v[...] = statistics(x_v[...])
         wait_all(w_copies)
         start_all(late)
         projection = ready_w if turn else out_w
@@ -345,7 +348,9 @@
             stores += start_all([pltpu.make_async_copy(grad_v, grad_out, sems.at[1])])
         if with_input:
             wait_all(late)
-            out_v[...] = input_gradient(upper_v, grad_v, x_v, qkv_w, gain_ref)
+            out_v[...] = input_gradient(
+                upper_v, grad_v, standard_v[...], inverse_v[...], qkv_w, gain_ref
+            )
             stores += start_all([pltpu.make_async_copy(out_v, input_out, sems.at[4])])
         wait_all(stores)
 
@@ -383,6 +388,8 @@
             pltpu.VMEM((width, 3 * INNER), BF16),
             pltpu.VMEM((length, width), BF16),
             pltpu.SemaphoreType.DMA((copy_count(layout, QKV_COLUMNS),)),
+            pltpu.VMEM((length, width), F32),
+            pltpu.VMEM((length, 1), F32),
         ]
     return call(
         body,
@@ -404,7 +411,7 @@
         copies = weight_copies(pieces, layout, w_v, w_sems, QKV_COLUMNS)
         copies.append(pltpu.make_async_copy(x, x_v, sems.at[0]))
         wait_all(start_all(copies))
-        out_v[...] = input_gradient(upper, grad, x_v, w_v, gain_ref)
+        out_v[...] = input_gradient(upper, grad, *statistics(x_v[...]), w_v, gain_ref)
         wait_all(start_all([pltpu.make_async_copy(out_v, out, sems.at[1])]))
 
 

time: 121 us -> 121 us (level)
  no operation moved by 1% of the time
where the time goes in v3:
time: 121 us
  waiting for transfers between devices  53.4 us (44%)
  starting transfers between devices  32.1 us (27%)
  Pallas kernels  29.7 us (25%)
  other arithmetic  2.24 us (2%)
  local copies, waits for them, and re-layouts  2.19 us (2%)
    ppermute x22, waiting for transfers between devices, across(): lax.ppermute(value, 'dp', [(source, source ^ bit) for source in range(cou...  50.9 us
    ppermute x22, starting transfers between devices, across(): lax.ppermute(value, 'dp', [(source, source ^ bit) for source in range(cou...  30.8 us
    pallas_call x4, Pallas kernels, forward(): call(body, (shape((HEADS, length, length)), shape((length, INNER)), shape...  11.6 us
    pallas_call x2, Pallas kernels, section_backward(): call(body, tuple(outs), specs + [ANY] * (len(inputs) - len(specs)), (VMEM...  9.47 us
    pallas_call x1, Pallas kernels, project(): call(body, shape((length, width)), [VMEM] * 3 + [ANY] * (len(inputs) - 3)...  4.89 us
    pallas_call x2, Pallas kernels, weight_terms(): call(bound, tuple((shape(each) for each in dims)), [VMEM] * len(inputs),...  2.65 us
    ppermute x1, waiting for transfers between devices, on_device(): lax.ppermute(carry[2], 'pipe', [(source, source - 1) for source in range(...  2.58 us
  transfers between devices with their start and end apart: 23, of which 16 were waited for; matrix products, arithmetic and copies ran while one was open for 1% of the time, Pallas kernels for 5%

profile of v3, /device:TPU:0, one launch (start us, length us, event | category | flops | bytes accessed | tf_op | source)
XLA Modules:
  0.0 120.5 jit_solution(12660628513842796707)
XLA Ops:
  0.7 1.0 copy.18
  1.6 11.3 %shard_map.77 = (bf16[12,512,512]{2,1,0:T(8,128)(2,1)S(1)}, bf16[512,768]{1,0:T(8,128)(2,1)S(1)}, bf16[512,2304]{1,0:T(8,128)(2,1)S(1)}) custom-call(s32[12,6,3]{2,1,0:T(8,128)S(1)} %bitcast.17, bf16[512,2304]{1,0:T(8,128)(2,1)} %bitcast.5), custom_call_target="tpu_custom_call" | custom-call | tf_op jit(solution)/shard_map/pallas_call | solution.py:167
  13.0 4.1 %collective-permute-start = (bf16[1,48,3072]{2,1,0:T(8,128)(2,1)}, bf16[1,48,3072]{2,1,0:T(8,128)(2,1)S(1)}, u32[]{:S(2)}, u32[]{:S(2)}) collective-permute-start(bf16[1,48,3072]{2,1,0:T(8,128)(2,1)} %param.9), channel_id=1, source_target_pairs={{0,8},{1,9},{2,10},{3,11},{4,12},{5,13},{6,14},{7,15},{8,0},{9,1},... | collective-permute-start | bytes 884744 | tf_op jit(solution)/shard_map/ppermute | solution.py:549
  17.1 1.1 copy-done.2
  18.2 0.7 shard_map.79.refs_0_
  19.0 6.3 %collective-permute-done = bf16[1,48,3072]{2,1,0:T(8,128)(2,1)S(1)} collective-permute-done((bf16[1,48,3072]{2,1,0:T(8,128)(2,1)}, bf16[1,48,3072]{2,1,0:T(8,128)(2,1)S(1)}, u32[]{:S(2)}, u32[]{:S(2)}) %collective-permute-start) | collective-permute-done | bytes 294944 | tf_op jit(solution)/shard_map/ppermute | solution.py:549
  25.4 1.1 collective-permute-start.5
  26.5 1.5 %collective-permute-start.3 = (bf16[2,48,1024]{2,1,0:T(8,128)(2,1)S(1)}, bf16[2,48,1024]{2,1,0:T(8,128)(2,1)S(1)}, u32[]{:S(2)}, u32[]{:S(2)}) collective-permute-start(bf16[2,48,1024]{2,1,0:T(8,128)(2,1)S(1)} %get-tuple-element.91), channel_id=1, source_target_pairs={{0,2},{1,3},{2,0},{3,1},{4,6},{5,7},{6,4},{7,5},{8,10},{9,11},{10,... | collective-permute-start | bytes 589832 | tf_op jit(solution)/shard_map/ppermute | solution.py:549
  28.0 1.5 %collective-permute-start.1 = (bf16[2,48,1024]{2,1,0:T(8,128)(2,1)S(1)}, bf16[2,48,1024]{2,1,0:T(8,128)(2,1)S(1)}, u32[]{:S(2)}, u32[]{:S(2)}) collective-permute-start(bf16[2,48,1024]{2,1,0:T(8,128)(2,1)S(1)} %get-tuple-element.92), channel_id=1, source_target_pairs={{0,1},{1,0},{2,3},{3,2},{4,5},{5,4},{6,7},{7,6},{8,9},{9,8},{10,11... | collective-permute-start | bytes 589832 | tf_op jit(solution)/shard_map/ppermute | solution.py:549
  29.5 2.4 %collective-permute-done.5 = bf16[2,48,1024]{2,1,0:T(8,128)(2,1)S(1)} collective-permute-done((bf16[2,48,1024]{2,1,0:T(8,128)(2,1)S(1)}, bf16[2,48,1024]{2,1,0:T(8,128)(2,1)S(1)}, u32[]{:S(2)}, u32[]{:S(2)}) %collective-permute-start.5) | collective-permute-done | bytes 196640 | tf_op jit(solution)/shard_map/ppermute | solution.py:549
  31.9 2.5 %collective-permute-start.6 = (bf16[4,48,1024]{2,1,0:T(8,128)(2,1)S(1)}, bf16[4,48,1024]{2,1,0:T(8,128)(2,1)S(1)}, u32[]{:S(2)}, u32[]{:S(2)}) collective-permute-start(bf16[4,48,1024]{2,1,0:T(8,128)(2,1)S(1)} %pad_maximum_fusion.6), channel_id=1, source_target_pairs={{0,1},{1,0},{2,3},{3,2},{4,5},{5,4},{6,7},{7,6},{8,9},{9,8},{10,11... | collective-permute-start | bytes 1179656 | tf_op jit(solution)/shard_map/ppermute | solution.py:549
  34.4 0.7 collective-permute-start.4
  35.1 0.6 collective-permute-done.1
  35.8 0.9 collective-permute-start.2
  36.8 7.6 %collective-permute-done.6 = bf16[4,48,1024]{2,1,0:T(8,128)(2,1)S(1)} collective-permute-done((bf16[4,48,1024]{2,1,0:T(8,128)(2,1)S(1)}, bf16[4,48,1024]{2,1,0:T(8,128)(2,1)S(1)}, u32[]{:S(2)}, u32[]{:S(2)}) %collective-permute-start.6) | collective-permute-done | bytes 393248 | tf_op jit(solution)/shard_map/ppermute | solution.py:549
  44.6 0.2 collective-permute-done.2
  44.9 1.1 collective-permute-start.7
  45.9 1.8 %collective-permute-start.8 = (bf16[8,48,1024]{2,1,0:T(8,128)(2,1)S(1)}, bf16[8,48,1024]{2,1,0:T(8,128)(2,1)S(1)}, u32[]{:S(2)}, u32[]{:S(2)}) collective-permute-start(bf16[8,48,1024]{2,1,0:T(8,128)(2,1)S(1)} %pad_maximum_fusion.1.refs_10_.refs_2_.refs_6_), channel_id=1, source_target_pairs={{0,1},{1,0},{2,3},{3,2},{4,5},{5,4},{6,7},{7,6},{8,9},{9,8},{10,11... | collective-permute-start | bytes 2359304 | tf_op jit(solution)/shard_map/ppermute | solution.py:549
  47.7 1.5 %collective-permute-start.9 = (bf16[8,48,1024]{2,1,0:T(8,128)(2,1)S(1)}, bf16[8,48,1024]{2,1,0:T(8,128)(2,1)S(1)}, u32[]{:S(2)}, u32[]{:S(2)}) collective-permute-start(bf16[8,48,1024]{2,1,0:T(8,128)(2,1)S(1)} %pad_maximum_fusion.2.refs_12_.refs_4_.refs_8_), channel_id=1, source_target_pairs={{0,2},{1,3},{2,0},{3,1},{4,6},{5,7},{6,4},{7,5},{8,10},{9,11},{10,... | collective-permute-start | bytes 2359304 | tf_op jit(solution)/shard_map/ppermute | solution.py:549
  49.4 7.6 %collective-permute-done.7.refs_9_.refs_1_.refs_5_ = bf16[8,48,1024]{2,1,0:T(8,128)(2,1)S(1)} collective-permute-done((bf16[8,48,1024]{2,1,0:T(8,128)(2,1)S(1)}, bf16[8,48,1024]{2,1,0:T(8,128)(2,1)S(1)}, u32[]{:S(2)}, u32[]{:S(2)}) %collective-permute-start.7) | collective-permute-done | bytes 786464 | tf_op jit(solution)/shard_map/ppermute | solution.py:549
  56.9 1.0 collective-permute-done.8.refs_11_.refs_3_.refs_7_
  57.9 1.8 %collective-permute-done.9.refs_13_.refs_5_.refs_9_ = bf16[8,48,1024]{2,1,0:T(8,128)(2,1)S(1)} collective-permute-done((bf16[8,48,1024]{2,1,0:T(8,128)(2,1)S(1)}, bf16[8,48,1024]{2,1,0:T(8,128)(2,1)S(1)}, u32[]{:S(2)}, u32[]{:S(2)}) %collective-permute-start.9) | collective-permute-done | bytes 786464 | tf_op jit(solution)/shard_map/ppermute | solution.py:549
  59.7 0.6 shard_map.82
  60.4 1.3 %collective-permute-start.10 = (bf16[512,768]{1,0:T(8,128)(2,1)}, bf16[512,768]{1,0:T(8,128)(2,1)S(1)}, u32[]{:S(2)}, u32[]{:S(2)}) collective-permute-start(bf16[512,768]{1,0:T(8,128)(2,1)} %get-tuple-element.72.refs_10_), channel_id=1, source_target_pairs={{16,0},{17,1},{18,2},{19,3},{20,4},{21,5},{22,6},{23,7},{24,8},{25... | collective-permute-start | bytes 2359304 | tf_op jit(solution)/shard_map/ppermute | solution.py:644
  61.7 0.5 shard_map.83.refs_7_
  62.2 2.6 %collective-permute-done.10.refs_1_ = bf16[512,768]{1,0:T(8,128)(2,1)S(1)} collective-permute-done((bf16[512,768]{1,0:T(8,128)(2,1)}, bf16[512,768]{1,0:T(8,128)(2,1)S(1)}, u32[]{:S(2)}, u32[]{:S(2)}) %collective-permute-start.10) | collective-permute-done | bytes 786464 | tf_op jit(solution)/shard_map/ppermute | solution.py:644
  64.8 8.9 %shard_map.84 = (bf16[512,768]{1,0:T(8,128)(2,1)S(1)}, bf16[512,2304]{1,0:T(8,128)(2,1)S(1)}) custom-call(f32[1,768]{1,0:T(1,128)S(1)} %copy-done.4, bf16[512,768]{1,0:T(8,128)(2,1)S(1)} %collective-permute-done.10.refs_1_, bf16[512,768]{1,0:T(8,128)(2,1)S(1)} %bitcast.12, bf16[512,768]{1,0:T(8,128)(2,1)S(1)} %bitcast.15, ...), custom_call_target="tpu_custom_call" | custom-call | tf_op jit(solution)/shard_map/pallas_call | solution.py:394
  73.6 2.6 %shard_map.87 = (bf16[8,48,1024]{2,1,0:T(8,128)(2,1)S(1)}, bf16[8,48,1024]{2,1,0:T(8,128)(2,1)S(1)}, bf16[8,48,1024]{2,1,0:T(8,128)(2,1)S(1)}, bf16[8,48,1024]{2...) custom-call(bf16[768,512]{1,0:T(8,128)(2,1)S(1)} %shard_map.79.refs_0_, ...), custom_call_target="tpu_custom_call" | custom-call | tf_op jit(solution)/shard_map/pallas_call | solution.py:512
  76.3 0.3 collective-permute-start.11
  76.6 1.8 %collective-permute-start.15 = (bf16[8,48,1024]{2,1,0:T(8,128)(2,1)S(1)}, bf16[8,48,1024]{2,1,0:T(8,128)(2,1)S(1)}, u32[]{:S(2)}, u32[]{:S(2)}) collective-permute-start(bf16[8,48,1024]{2,1,0:T(8,128)(2,1)S(1)} %get-tuple-element.87), channel_id=1, source_target_pairs={{0,2},{1,3},{2,0},{3,1},{4,6},{5,7},{6,4},{7,5},{8,10},{9,11},{10,... | collective-permute-start | bytes 2359304 | tf_op jit(solution)/shard_map/ppermute | solution.py:549
  78.4 0.8 collective-permute-start.19
  79.2 4.9 %shard_map.85 = bf16[512,768]{1,0:T(8,128)(2,1)} custom-call(f32[1,768]{1,0:T(1,128)S(1)} %copy-done.4, bf16[512,768]{1,0:T(8,128)(2,1)S(1)} %get-tuple-element.73.refs_1_, bf16[512,2304]{1,0:T(8,128)(2,1)S(1)} %get-tuple-element.74.refs_2_, bf16[512,768]{1,0:T(8,128)(2,1)S(1)} %bitcast.16, ...), custom_call_target="tpu_custom_call", output_to_operand_aliasing={{}: (10, {})} | custom-call | tf_op jit(solution)/shard_map/pallas_call | solution.py:425
  84.1 8.8 %collective-permute-done.11 = bf16[8,48,1024]{2,1,0:T(8,128)(2,1)S(1)} collective-permute-done((bf16[8,48,1024]{2,1,0:T(8,128)(2,1)S(1)}, bf16[8,48,1024]{2,1,0:T(8,128)(2,1)S(1)}, u32[]{:S(2)}, u32[]{:S(2)}) %collective-permute-start.11) | collective-permute-done | bytes 786464 | tf_op jit(solution)/shard_map/ppermute | solution.py:549
  93.1 1.8 %collective-permute-start.12 = (bf16[4,48,1024]{2,1,0:T(8,128)(2,1)S(1)}, bf16[4,48,1024]{2,1,0:T(8,128)(2,1)S(1)}, u32[]{:S(2)}, u32[]{:S(2)}) collective-permute-start(bf16[4,48,1024]{2,1,0:T(8,128)(2,1)S(1)} %add_convert_fusion.2), channel_id=1, source_target_pairs={{0,2},{1,3},{2,0},{3,1},{4,6},{5,7},{6,4},{7,5},{8,10},{9,11},{10,... | collective-permute-start | bytes 1179656 | tf_op jit(solution)/shard_map/ppermute | solution.py:549
  95.0 1.4 %collective-permute-start.16 = (bf16[4,48,1024]{2,1,0:T(8,128)(2,1)S(1)}, bf16[4,48,1024]{2,1,0:T(8,128)(2,1)S(1)}, u32[]{:S(2)}, u32[]{:S(2)}) collective-permute-start(bf16[4,48,1024]{2,1,0:T(8,128)(2,1)S(1)} %add_convert_fusion.1), channel_id=1, source_target_pairs={{0,4},{1,5},{2,6},{3,7},{4,0},{5,1},{6,2},{7,3},{8,12},{9,13},{10,... | collective-permute-start | bytes 1179656 | tf_op jit(solution)/shard_map/ppermute | solution.py:549
  96.6 0.3 collective-permute-start.20
  96.8 4.1 %collective-permute-done.12 = bf16[4,48,1024]{2,1,0:T(8,128)(2,1)S(1)} collective-permute-done((bf16[4,48,1024]{2,1,0:T(8,128)(2,1)S(1)}, bf16[4,48,1024]{2,1,0:T(8,128)(2,1)S(1)}, u32[]{:S(2)}, u32[]{:S(2)}) %collective-permute-start.12) | collective-permute-done | bytes 393248 | tf_op jit(solution)/shard_map/ppermute | solution.py:549
  101.0 1.2 collective-permute-start.13
  102.1 3.9 %collective-permute-done.16 = bf16[4,48,1024]{2,1,0:T(8,128)(2,1)S(1)} collective-permute-done((bf16[4,48,1024]{2,1,0:T(8,128)(2,1)S(1)}, bf16[4,48,1024]{2,1,0:T(8,128)(2,1)S(1)}, u32[]{:S(2)}, u32[]{:S(2)}) %collective-permute-start.16) | collective-permute-done | bytes 393248 | tf_op jit(solution)/shard_map/ppermute | solution.py:549
  106.1 0.9 collective-permute-start.17
  107.1 1.0 collective-permute-done.13
  108.2 2.5 %collective-permute-start.14 = (bf16[1,48,1024]{2,1,0:T(8,128)(2,1)S(1)}, bf16[1,48,1024]{2,1,0:T(8,128)(2,1)S(1)}, u32[]{:S(2)}, u32[]{:S(2)}) collective-permute-start(bf16[1,48,1024]{2,1,0:T(8,128)(2,1)S(1)} %add_convert_fusion.8), channel_id=1, source_target_pairs={{0,8},{1,9},{2,10},{3,11},{4,12},{5,13},{6,14},{7,15},{8,0},{9,1},... | collective-permute-start | bytes 294920 | tf_op jit(solution)/shard_map/ppermute | solution.py:549
  110.6 1.2 collective-permute-done.17
  111.9 2.1 %collective-permute-start.18 = (bf16[1,48,1024]{2,1,0:T(8,128)(2,1)S(1)}, bf16[1,48,1024]{2,1,0:T(8,128)(2,1)S(1)}, u32[]{:S(2)}, u32[]{:S(2)}) collective-permute-start(bf16[1,48,1024]{2,1,0:T(8,128)(2,1)S(1)} %add_convert_fusion.7), channel_id=1, source_target_pairs={{0,8},{1,9},{2,10},{3,11},{4,12},{5,13},{6,14},{7,15},{8,0},{9,1},... | collective-permute-start | bytes 294920 | tf_op jit(solution)/shard_map/ppermute | solution.py:549
  114.0 1.0 collective-permute-start.22
  115.1 2.4 %collective-permute-done.18 = bf16[1,48,1024]{2,1,0:T(8,128)(2,1)S(1)} collective-permute-done((bf16[1,48,1024]{2,1,0:T(8,128)(2,1)S(1)}, bf16[1,48,1024]{2,1,0:T(8,128)(2,1)S(1)}, u32[]{:S(2)}, u32[]{:S(2)}) %collective-permute-start.18) | collective-permute-done | bytes 98336 | tf_op jit(solution)/shard_map/ppermute | solution.py:549
  117.5 2.1 %collective-permute-done.22 = bf16[1,48,1024]{2,1,0:T(8,128)(2,1)S(1)} collective-permute-done((bf16[1,48,1024]{2,1,0:T(8,128)(2,1)S(1)}, bf16[1,48,1024]{2,1,0:T(8,128)(2,1)S(1)}, u32[]{:S(2)}, u32[]{:S(2)}) %collective-permute-start.22) | collective-permute-done | bytes 98336 | tf_op jit(solution)/shard_map/ppermute | solution.py:549
  119.7 0.9 maximum_multiply_fusion
  (43 shorter events, 1.8 us)
Async XLA Ops:
  0.6 18.2 %copy-start = (bf16[1,1,512,2304]{3,2,1,0:T(8,128)(2,1)S(1)}, bf16[1,1,512,2304]{3,2,1,0:T(8,128)(2,1)}, u32[]{:S(2)}) copy-start(bf16[1,1,512,2304]{3,2,1,0:T(8,128)(2,1)} %param.7) | copy-start | bytes 7077892
  0.6 16.4 %copy-start.4 = (f32[1,768]{1,0:T(1,128)S(1)}, f32[1,768]{1,0:T(1,128)}, u32[]{:S(2)}) copy-start(f32[1,768]{1,0:T(1,128)} %refs_0_.5) | copy-start | bytes 9220
  13.0 12.3 %collective-permute-start = (bf16[1,48,3072]{2,1,0:T(8,128)(2,1)}, bf16[1,48,3072]{2,1,0:T(8,128)(2,1)S(1)}, u32[]{:S(2)}, u32[]{:S(2)}) collective-permute-start(bf16[1,48,3072]{2,1,0:T(8,128)(2,1)} %param.9), channel_id=1, source_target_pairs={{0,8},{1,9},{2,10},{3,11},{4,12},{5,13},{6,14},{7,15},{8,0},{9,1},... | collective-permute-start | bytes 884744 | tf_op jit(solution)/shard_map/ppermute | solution.py:549
  17.1 1.1 copy-start.2
  18.9 6.4 %copy-start.5 = (bf16[1,48,3072]{2,1,0:T(8,128)(2,1)S(1)}, bf16[1,48,3072]{2,1,0:T(8,128)(2,1)}, u32[]{:S(2)}) copy-start(bf16[1,48,3072]{2,1,0:T(8,128)(2,1)} %param.9) | copy-start | bytes 884740
  25.4 6.5 %collective-permute-start.5 = (bf16[2,48,1024]{2,1,0:T(8,128)(2,1)S(1)}, bf16[2,48,1024]{2,1,0:T(8,128)(2,1)S(1)}, u32[]{:S(2)}, u32[]{:S(2)}) collective-permute-start(bf16[2,48,1024]{2,1,0:T(8,128)(2,1)S(1)} %get-tuple-element.90), channel_id=1, source_target_pairs={{0,4},{1,5},{2,6},{3,7},{4,0},{5,1},{6,2},{7,3},{8,12},{9,13},{10,... | collective-permute-start | bytes 589832 | tf_op jit(solution)/shard_map/ppermute | solution.py:549
  26.5 7.9 %collective-permute-start.3 = (bf16[2,48,1024]{2,1,0:T(8,128)(2,1)S(1)}, bf16[2,48,1024]{2,1,0:T(8,128)(2,1)S(1)}, u32[]{:S(2)}, u32[]{:S(2)}) collective-permute-start(bf16[2,48,1024]{2,1,0:T(8,128)(2,1)S(1)} %get-tuple-element.91), channel_id=1, source_target_pairs={{0,2},{1,3},{2,0},{3,1},{4,6},{5,7},{6,4},{7,5},{8,10},{9,11},{10,... | collective-permute-start | bytes 589832 | tf_op jit(solution)/shard_map/ppermute | solution.py:549
  28.0 7.8 %collective-permute-start.1 = (bf16[2,48,1024]{2,1,0:T(8,128)(2,1)S(1)}, bf16[2,48,1024]{2,1,0:T(8,128)(2,1)S(1)}, u32[]{:S(2)}, u32[]{:S(2)}) collective-permute-start(bf16[2,48,1024]{2,1,0:T(8,128)(2,1)S(1)} %get-tuple-element.92), channel_id=1, source_target_pairs={{0,1},{1,0},{2,3},{3,2},{4,5},{5,4},{6,7},{7,6},{8,9},{9,8},{10,11... | collective-permute-start | bytes 589832 | tf_op jit(solution)/shard_map/ppermute | solution.py:549
  31.9 12.5 %collective-permute-start.6 = (bf16[4,48,1024]{2,1,0:T(8,128)(2,1)S(1)}, bf16[4,48,1024]{2,1,0:T(8,128)(2,1)S(1)}, u32[]{:S(2)}, u32[]{:S(2)}) collective-permute-start(bf16[4,48,1024]{2,1,0:T(8,128)(2,1)S(1)} %pad_maximum_fusion.6), channel_id=1, source_target_pairs={{0,1},{1,0},{2,3},{3,2},{4,5},{5,4},{6,7},{7,6},{8,9},{9,8},{10,11... | collective-permute-start | bytes 1179656 | tf_op jit(solution)/shard_map/ppermute | solution.py:549
  34.4 10.1 %collective-permute-start.4 = (bf16[4,48,1024]{2,1,0:T(8,128)(2,1)S(1)}, bf16[4,48,1024]{2,1,0:T(8,128)(2,1)S(1)}, u32[]{:S(2)}, u32[]{:S(2)}) collective-permute-start(bf16[4,48,1024]{2,1,0:T(8,128)(2,1)S(1)} %pad_maximum_fusion.5), channel_id=1, source_target_pairs={{0,4},{1,5},{2,6},{3,7},{4,0},{5,1},{6,2},{7,3},{8,12},{9,13},{10,... | collective-permute-start | bytes 1179656 | tf_op jit(solution)/shard_map/ppermute | solution.py:549
  35.8 9.0 %collective-permute-start.2 = (bf16[4,48,1024]{2,1,0:T(8,128)(2,1)S(1)}, bf16[4,48,1024]{2,1,0:T(8,128)(2,1)S(1)}, u32[]{:S(2)}, u32[]{:S(2)}) collective-permute-start(bf16[4,48,1024]{2,1,0:T(8,128)(2,1)S(1)} %pad_maximum_fusion.4), channel_id=1, source_target_pairs={{0,2},{1,3},{2,0},{3,1},{4,6},{5,7},{6,4},{7,5},{8,10},{9,11},{10,... | collective-permute-start | bytes 1179656 | tf_op jit(solution)/shard_map/ppermute | solution.py:549
  44.9 14.9 %copy-start.1 = (bf16[1,512,768]{2,1,0:T(8,128)(2,1)S(1)}, bf16[1,512,768]{2,1,0:T(8,128)(2,1)}, u32[]{:S(2)}) copy-start(bf16[1,512,768]{2,1,0:T(8,128)(2,1)} %param.11) | copy-start | bytes 2359300
  44.9 14.9 %copy-start.3 = (bf16[1,1,512,768]{3,2,1,0:T(8,128)(2,1)S(1)}, bf16[1,1,512,768]{3,2,1,0:T(8,128)(2,1)}, u32[]{:S(2)}) copy-start(bf16[1,1,512,768]{3,2,1,0:T(8,128)(2,1)} %param.6) | copy-start | bytes 2359300
  44.9 12.1 %collective-permute-start.7 = (bf16[8,48,1024]{2,1,0:T(8,128)(2,1)S(1)}, bf16[8,48,1024]{2,1,0:T(8,128)(2,1)S(1)}, u32[]{:S(2)}, u32[]{:S(2)}) collective-permute-start(bf16[8,48,1024]{2,1,0:T(8,128)(2,1)S(1)} %pad_maximum_fusion.refs_8_.refs_0_.refs_4_), channel_id=1, source_target_pairs={{0,4},{1,5},{2,6},{3,7},{4,0},{5,1},{6,2},{7,3},{8,12},{9,13},{10,... | collective-permute-start | bytes 2359304 | tf_op jit(solution)/shard_map/ppermute | solution.py:549
  45.9 12.0 %collective-permute-start.8 = (bf16[8,48,1024]{2,1,0:T(8,128)(2,1)S(1)}, bf16[8,48,1024]{2,1,0:T(8,128)(2,1)S(1)}, u32[]{:S(2)}, u32[]{:S(2)}) collective-permute-start(bf16[8,48,1024]{2,1,0:T(8,128)(2,1)S(1)} %pad_maximum_fusion.1.refs_10_.refs_2_.refs_6_), channel_id=1, source_target_pairs={{0,1},{1,0},{2,3},{3,2},{4,5},{5,4},{6,7},{7,6},{8,9},{9,8},{10,11... | collective-permute-start | bytes 2359304 | tf_op jit(solution)/shard_map/ppermute | solution.py:549
  47.7 12.0 %collective-permute-start.9 = (bf16[8,48,1024]{2,1,0:T(8,128)(2,1)S(1)}, bf16[8,48,1024]{2,1,0:T(8,128)(2,1)S(1)}, u32[]{:S(2)}, u32[]{:S(2)}) collective-permute-start(bf16[8,48,1024]{2,1,0:T(8,128)(2,1)S(1)} %pad_maximum_fusion.2.refs_12_.refs_4_.refs_8_), channel_id=1, source_target_pairs={{0,2},{1,3},{2,0},{3,1},{4,6},{5,7},{6,4},{7,5},{8,10},{9,11},{10,... | collective-permute-start | bytes 2359304 | tf_op jit(solution)/shard_map/ppermute | solution.py:549
  60.4 4.4 %collective-permute-start.10 = (bf16[512,768]{1,0:T(8,128)(2,1)}, bf16[512,768]{1,0:T(8,128)(2,1)S(1)}, u32[]{:S(2)}, u32[]{:S(2)}) collective-permute-start(bf16[512,768]{1,0:T(8,128)(2,1)} %get-tuple-element.72.refs_10_), channel_id=1, source_target_pairs={{16,0},{17,1},{18,2},{19,3},{20,4},{21,5},{22,6},{23,7},{24,8},{25... | collective-permute-start | bytes 2359304 | tf_op jit(solution)/shard_map/ppermute | solution.py:644
  76.3 16.7 %collective-permute-start.11 = (bf16[8,48,1024]{2,1,0:T(8,128)(2,1)S(1)}, bf16[8,48,1024]{2,1,0:T(8,128)(2,1)S(1)}, u32[]{:S(2)}, u32[]{:S(2)}) collective-permute-start(bf16[8,48,1024]{2,1,0:T(8,128)(2,1)S(1)} %get-tuple-element.85), channel_id=1, source_target_pairs={{0,1},{1,0},{2,3},{3,2},{4,5},{5,4},{6,7},{7,6},{8,9},{9,8},{10,11... | collective-permute-start | bytes 2359304 | tf_op jit(solution)/shard_map/ppermute | solution.py:549
  76.6 18.3 %collective-permute-start.15 = (bf16[8,48,1024]{2,1,0:T(8,128)(2,1)S(1)}, bf16[8,48,1024]{2,1,0:T(8,128)(2,1)S(1)}, u32[]{:S(2)}, u32[]{:S(2)}) collective-permute-start(bf16[8,48,1024]{2,1,0:T(8,128)(2,1)S(1)} %get-tuple-element.87), channel_id=1, source_target_pairs={{0,2},{1,3},{2,0},{3,1},{4,6},{5,7},{6,4},{7,5},{8,10},{9,11},{10,... | collective-permute-start | bytes 2359304 | tf_op jit(solution)/shard_map/ppermute | solution.py:549
  78.4 18.0 %collective-permute-start.19 = (bf16[8,48,1024]{2,1,0:T(8,128)(2,1)S(1)}, bf16[8,48,1024]{2,1,0:T(8,128)(2,1)S(1)}, u32[]{:S(2)}, u32[]{:S(2)}) collective-permute-start(bf16[8,48,1024]{2,1,0:T(8,128)(2,1)S(1)} %get-tuple-element.89), channel_id=1, source_target_pairs={{0,4},{1,5},{2,6},{3,7},{4,0},{5,1},{6,2},{7,3},{8,12},{9,13},{10,... | collective-permute-start | bytes 2359304 | tf_op jit(solution)/shard_map/ppermute | solution.py:549
  93.1 7.8 %collective-permute-start.12 = (bf16[4,48,1024]{2,1,0:T(8,128)(2,1)S(1)}, bf16[4,48,1024]{2,1,0:T(8,128)(2,1)S(1)}, u32[]{:S(2)}, u32[]{:S(2)}) collective-permute-start(bf16[4,48,1024]{2,1,0:T(8,128)(2,1)S(1)} %add_convert_fusion.2), channel_id=1, source_target_pairs={{0,2},{1,3},{2,0},{3,1},{4,6},{5,7},{6,4},{7,5},{8,10},{9,11},{10,... | collective-permute-start | bytes 1179656 | tf_op jit(solution)/shard_map/ppermute | solution.py:549
  95.0 11.0 %collective-permute-start.16 = (bf16[4,48,1024]{2,1,0:T(8,128)(2,1)S(1)}, bf16[4,48,1024]{2,1,0:T(8,128)(2,1)S(1)}, u32[]{:S(2)}, u32[]{:S(2)}) collective-permute-start(bf16[4,48,1024]{2,1,0:T(8,128)(2,1)S(1)} %add_convert_fusion.1), channel_id=1, source_target_pairs={{0,4},{1,5},{2,6},{3,7},{4,0},{5,1},{6,2},{7,3},{8,12},{9,13},{10,... | collective-permute-start | bytes 1179656 | tf_op jit(solution)/shard_map/ppermute | solution.py:549
  96.6 10.4 %collective-permute-start.20 = (bf16[4,48,1024]{2,1,0:T(8,128)(2,1)S(1)}, bf16[4,48,1024]{2,1,0:T(8,128)(2,1)S(1)}, u32[]{:S(2)}, u32[]{:S(2)}) collective-permute-start(bf16[4,48,1024]{2,1,0:T(8,128)(2,1)S(1)} %add_convert_fusion), channel_id=1, source_target_pairs={{0,1},{1,0},{2,3},{3,2},{4,5},{5,4},{6,7},{7,6},{8,9},{9,8},{10,11... | collective-permute-start | bytes 1179656 | tf_op jit(solution)/shard_map/ppermute | solution.py:549
  101.0 7.1 %collective-permute-start.13 = (bf16[2,48,1024]{2,1,0:T(8,128)(2,1)S(1)}, bf16[2,48,1024]{2,1,0:T(8,128)(2,1)S(1)}, u32[]{:S(2)}, u32[]{:S(2)}) collective-permute-start(bf16[2,48,1024]{2,1,0:T(8,128)(2,1)S(1)} %add_convert_fusion.5), channel_id=1, source_target_pairs={{0,4},{1,5},{2,6},{3,7},{4,0},{5,1},{6,2},{7,3},{8,12},{9,13},{10,... | collective-permute-start | bytes 589832 | tf_op jit(solution)/shard_map/ppermute | solution.py:549
  106.1 5.7 %collective-permute-start.17 = (bf16[2,48,1024]{2,1,0:T(8,128)(2,1)S(1)}, bf16[2,48,1024]{2,1,0:T(8,128)(2,1)S(1)}, u32[]{:S(2)}, u32[]{:S(2)}) collective-permute-start(bf16[2,48,1024]{2,1,0:T(8,128)(2,1)S(1)} %add_convert_fusion.4), channel_id=1, source_target_pairs={{0,1},{1,0},{2,3},{3,2},{4,5},{5,4},{6,7},{7,6},{8,9},{9,8},{10,11... | collective-permute-start | bytes 589832 | tf_op jit(solution)/shard_map/ppermute | solution.py:549
  107.0 7.0 %collective-permute-start.21 = (bf16[2,48,1024]{2,1,0:T(8,128)(2,1)S(1)}, bf16[2,48,1024]{2,1,0:T(8,128)(2,1)S(1)}, u32[]{:S(2)}, u32[]{:S(2)}) collective-permute-start(bf16[2,48,1024]{2,1,0:T(8,128)(2,1)S(1)} %add_convert_fusion.3), channel_id=1, source_target_pairs={{0,2},{1,3},{2,0},{3,1},{4,6},{5,7},{6,4},{7,5},{8,10},{9,11},{10,... | collective-permute-start | bytes 589832 | tf_op jit(solution)/shard_map/ppermute | solution.py:549
  108.2 6.8 %collective-permute-start.14 = (bf16[1,48,1024]{2,1,0:T(8,128)(2,1)S(1)}, bf16[1,48,1024]{2,1,0:T(8,128)(2,1)S(1)}, u32[]{:S(2)}, u32[]{:S(2)}) collective-permute-start(bf16[1,48,1024]{2,1,0:T(8,128)(2,1)S(1)} %add_convert_fusion.8), channel_id=1, source_target_pairs={{0,8},{1,9},{2,10},{3,11},{4,12},{5,13},{6,14},{7,15},{8,0},{9,1},... | collective-permute-start | bytes 294920 | tf_op jit(solution)/shard_map/ppermute | solution.py:549
  111.9 5.6 %collective-permute-start.18 = (bf16[1,48,1024]{2,1,0:T(8,128)(2,1)S(1)}, bf16[1,48,1024]{2,1,0:T(8,128)(2,1)S(1)}, u32[]{:S(2)}, u32[]{:S(2)}) collective-permute-start(bf16[1,48,1024]{2,1,0:T(8,128)(2,1)S(1)} %add_convert_fusion.7), channel_id=1, source_target_pairs={{0,8},{1,9},{2,10},{3,11},{4,12},{5,13},{6,14},{7,15},{8,0},{9,1},... | collective-permute-start | bytes 294920 | tf_op jit(solution)/shard_map/ppermute | solution.py:549
  114.0 5.6 %collective-permute-start.22 = (bf16[1,48,1024]{2,1,0:T(8,128)(2,1)S(1)}, bf16[1,48,1024]{2,1,0:T(8,128)(2,1)S(1)}, u32[]{:S(2)}, u32[]{:S(2)}) collective-permute-start(bf16[1,48,1024]{2,1,0:T(8,128)(2,1)S(1)} %add_convert_fusion.6), channel_id=1, source_target_pairs={{0,8},{1,9},{2,10},{3,11},{4,12},{5,13},{6,14},{7,15},{8,0},{9,1},... | collective-permute-start | bytes 294920 | tf_op jit(solution)/shard_map/ppermute | solution.py:549
